TPU v7x, 256 devices: a whole 4x4x8 slice. The times are simulated.
256 devices in a mesh: tok: 64 (over x, z, core), head: 4 (over y).
Axes of the slice: x: 4, y: 4, z: 8, core: 2. Of those that a mesh axis runs over, the one named last changes fastest.
Arguments:
- queries: bfloat16 [2, 8192, 2048], P(None, 'tok', 'head'), may hold values from -16 to 16
- keys: bfloat16 [8192, 2048], P('tok', 'head'), may hold values from -16 to 16
- values: bfloat16 [8192, 2048], P('tok', 'head'), may hold values from -6 to 6
- upstream: bfloat16 [2, 8192, 2048], P(None, 'tok', 'head'), may hold values from -6 to 6
- out_gain: float32 [2048], P('head'), may hold values from 0.5 to 2
- gate_weight: bfloat16 [4, 512, 512], P('head', 'tok'), may hold values from -0.25 to 0.25
- up_weight: bfloat16 [4, 512, 512], P('head', 'tok'), may hold values from -0.25 to 0.25
- down_weight: bfloat16 [4, 512, 512], P('head', 'tok'), may hold values from -0.25 to 0.25
Outputs:
- grad_queries: bfloat16 [2, 8192, 2048], P(None, 'tok', 'head')
- grad_keys: bfloat16 [8192, 2048], P('tok', 'head')
- grad_values: bfloat16 [8192, 2048], P('tok', 'head')
- grad_gate: float32 [4, 512, 512], P('head', 'tok')
- grad_up: float32 [4, 512, 512], P('head', 'tok')
- grad_down: float32 [4, 512, 512], P('head', 'tok')
All inputs are finite; a program needn't handle non-finite values.
Results may differ from a plain program's by a relative error of at most 0.02.
Values may be sent and summed in bfloat16 or wider, within the bound.
A program may use at most 128 MiB of HBM per device.

v0:
```python
import math

import jax
import jax.numpy as jnp
from jax import lax
from jax.sharding import PartitionSpec as P

NS_STEPS = 2


lin_coef = 3.4445
cube_coef = -4.775
fifth_coef = 2.0315
rms_eps = 1e-06
fro_eps = 1e-07


def product(left, right):
    return jnp.dot(left, right, preferred_element_type=jnp.float32)


def across(left, right):
    return lax.dot_general(
        left, right, (((0,), (0,)), ((), ())), preferred_element_type=jnp.float32
    )


def against(left, right):
    return lax.dot_general(
        left, right, (((1,), (1,)), ((), ())), preferred_element_type=jnp.float32
    )


def fast_forward(keys, values, weights):
    gate_weight, up_weight, down_weight = weights
    gate_pre = product(keys, gate_weight)
    up_pre = product(keys, up_weight)
    sigma = jax.nn.sigmoid(gate_pre)
    active = gate_pre * sigma
    hidden = (active * up_pre).astype(jnp.bfloat16)
    back = -against(values, down_weight)
    slope = sigma * (1.0 + gate_pre * (1.0 - sigma))
    d_gate = (back * up_pre * slope).astype(jnp.bfloat16)
    d_up = (back * active).astype(jnp.bfloat16)
    fast = (across(keys, d_gate), across(keys, d_up), -across(hidden, values))
    saved = (gate_pre, up_pre, sigma, active, hidden, back, slope, d_gate, d_up)
    return (fast, saved)


def fast_second(keys, values, weights, saved, cots):
    gate_weight, up_weight, down_weight = weights
    gate_pre, up_pre, sigma, active, hidden, back, slope, d_gate, d_up = saved
    cot_gate, cot_up, cot_down = cots
    along_gate = product(keys, cot_gate)
    along_up = product(keys, cot_up)
    along_hidden = -against(values, cot_down)
    curve = sigma * (1.0 - sigma) * (2.0 + gate_pre * (1.0 - 2.0 * sigma))
    d_back = (along_gate * up_pre * slope + along_up * active).astype(jnp.bfloat16)
    d_upper = (along_gate * back * slope + along_hidden * active).astype(jnp.bfloat16)
    d_lower = (
        along_gate * back * up_pre * curve + along_up * back * slope + along_hidden * up_pre * slope
    ).astype(jnp.bfloat16)
    grad_keys = (
        against(d_gate, cot_gate)
        + against(d_up, cot_up)
        + against(d_lower, gate_weight)
        + against(d_upper, up_weight)
    ).astype(jnp.bfloat16)
    grad_values = (-product(hidden, cot_down) - product(d_back, down_weight)).astype(jnp.bfloat16)
    partial_value = (across(keys, d_lower), across(keys, d_upper), -across(d_back, values))
    return (grad_keys, grad_values, partial_value)


def apply_forward(queries, weights):
    gate_weight, up_weight, down_weight = weights
    gate_pre = product(queries, gate_weight)
    up_pre = product(queries, up_weight)
    sigma = jax.nn.sigmoid(gate_pre)
    hidden = (gate_pre * sigma * up_pre).astype(jnp.bfloat16)
    output = product(hidden, down_weight)
    return (gate_pre, up_pre, sigma, hidden, output)


def statistics(output, upstream, out_gain, width):
    weighted = out_gain * upstream.astype(jnp.float32)
    sums = lax.psum((jnp.sum(output * output, axis=1), jnp.sum(weighted * output, axis=1)), "head")
    return (lax.rsqrt(sums[0] / width + rms_eps), sums[1] / width)


def apply_backward(queries, weights, saved, upstream, out_gain, width):
    gate_weight, up_weight, down_weight = weights
    gate_pre, up_pre, sigma, hidden, output = saved
    inverse_rms, mean_dot = statistics(output, upstream, out_gain, width)
    weighted = out_gain * upstream.astype(jnp.float32)
    d_output = (
        inverse_rms[:, None] * weighted
        - output * (inverse_rms * inverse_rms * inverse_rms * mean_dot)[:, None]
    ).astype(jnp.bfloat16)
    back = against(d_output, down_weight)
    slope = sigma * (1.0 + gate_pre * (1.0 - sigma))
    d_gate = (back * up_pre * slope).astype(jnp.bfloat16)
    d_up = (back * gate_pre * sigma).astype(jnp.bfloat16)
    grad_queries = (against(d_gate, gate_weight) + against(d_up, up_weight)).astype(jnp.bfloat16)
    partial_value = (across(queries, d_gate), across(queries, d_up), across(hidden, d_output))
    return (grad_queries, partial_value)


def schulz_forward(begin):
    current = begin
    saved = []
    for sweep in range(NS_STEPS):
        gram = against(current, current).astype(jnp.bfloat16)
        blend = (cube_coef * gram.astype(jnp.float32) + fifth_coef * product(gram, gram)).astype(
            jnp.bfloat16
        )
        following = (lin_coef * current.astype(jnp.float32) + product(blend, current)).astype(
            jnp.bfloat16
        )
        saved.append((current, gram, blend))
        current = following
    return (current, saved)


def schulz_backward(cotan, saved):
    current = cotan
    for iterate, gram, blend in reversed(saved):
        cross = against(current, iterate)
        symmetric = (cross + cross.T).astype(jnp.bfloat16)
        bent = product(symmetric, gram)
        mixed = (cube_coef * symmetric.astype(jnp.float32) + fifth_coef * (bent + bent.T)).astype(
            jnp.bfloat16
        )
        current = (
            lin_coef * current.astype(jnp.float32)
            + product(blend, current)
            + product(mixed, iterate)
        ).astype(jnp.bfloat16)
    return current


def per_device(queries, keys, values, upstream, out_gain, gate_weight, up_weight, down_weight):
    shards = lax.axis_size("tok")
    owner = lax.axis_index("tok")
    width = out_gain.shape[0] * lax.axis_size("head")
    scale = 1.0 / math.sqrt(queries.shape[1] * shards)
    own_rows = (gate_weight[0], up_weight[0], down_weight[0])
    starts = [owner * own_rows[which].shape[0] for which in range(3)]
    first = (
        lax.all_gather(own_rows[0], "tok", axis=0, tiled=True),
        lax.all_gather(own_rows[1], "tok", axis=0, tiled=True),
        lax.all_gather(own_rows[2], "tok", axis=0, tiled=True),
    )
    fast, saved_keys = fast_forward(keys, values, first)
    apply_first = apply_forward(queries[0], first)
    grad_first, partial_first = apply_backward(
        queries[0], first, apply_first, upstream[0], out_gain, width
    )
    totals = lax.psum((fast[0], fast[1], fast[2]), "tok")
    roots = [jnp.sqrt(jnp.sum(totals[which] * totals[which])) for which in range(3)]
    forward = [
        schulz_forward((totals[which] / (roots[which] + fro_eps)).astype(jnp.bfloat16))
        for which in range(3)
    ]
    finals = [forward[which][0] for which in range(3)]
    second = tuple(
        (
            (first[which].astype(jnp.float32) - finals[which].astype(jnp.float32)).astype(
                jnp.bfloat16
            )
            for which in range(3)
        )
    )
    apply_second = apply_forward(queries[1], second)
    grad_second, partial_second = apply_backward(
        queries[1], second, apply_second, upstream[1], out_gain, width
    )
    rates = lax.psum((partial_second[0], partial_second[1], partial_second[2]), "tok")
    bottoms = [
        schulz_backward((-rates[which]).astype(jnp.bfloat16), forward[which][1])
        for which in range(3)
    ]
    cots = []
    for which in range(3):
        norm = roots[which] + fro_eps
        inner = jnp.sum(bottoms[which].astype(jnp.float32) * totals[which])
        cots.append(
            (
                bottoms[which].astype(jnp.float32) / norm
                - totals[which] * (inner / (norm * norm * roots[which]))
            ).astype(jnp.bfloat16)
        )
    rate_rows = [
        lax.dynamic_slice_in_dim(rates[which], starts[which], own_rows[which].shape[0], 0)
        for which in range(3)
    ]
    grad_keys, grad_values, second_order = fast_second(keys, values, first, saved_keys, cots)
    sums = (
        lax.psum_scatter(
            partial_first[0] + second_order[0], "tok", scatter_dimension=0, tiled=True
        ),
        lax.psum_scatter(
            partial_first[1] + second_order[1], "tok", scatter_dimension=0, tiled=True
        ),
        lax.psum_scatter(
            partial_first[2] + second_order[2], "tok", scatter_dimension=0, tiled=True
        ),
    )
    grad_gate = ((sums[0] + rate_rows[0]) * scale)[None]
    grad_up = ((sums[1] + rate_rows[1]) * scale)[None]
    grad_down = ((sums[2] + rate_rows[2]) * scale)[None]
    grad_queries = jnp.stack([grad_first, grad_second])
    return (grad_queries, grad_keys, grad_values, grad_gate, grad_up, grad_down)


def solution(mesh):
    in_specs = (
        P(None, "tok", "head"),
        P("tok", "head"),
        P("tok", "head"),
        P(None, "tok", "head"),
        P("head"),
        P("head", "tok", None),
        P("head", "tok", None),
        P("head", "tok", None),
    )
    out_specs = (
        P(None, "tok", "head"),
        P("tok", "head"),
        P("tok", "head"),
        P("head", "tok", None),
        P("head", "tok", None),
        P("head", "tok", None),
    )
    return jax.shard_map(
        per_device, mesh=mesh, in_specs=in_specs, out_specs=out_specs, check_vma=False
    )
```

profile of v0, /device:TPU:1, one launch (start us, length us, event | category | flops | bytes accessed | tf_op | source)
XLA Modules:
  0.0 1130.9 jit_solution(10835314642906359188)
XLA Ops:
  7.2 54.9 %all-gather = bf16[1,512,512]{2,1,0:T(8,128)(2,1)S(1)} all-gather(bf16[1,8,512]{2,1,0:T(8,128)(2,1)} %param.13), channel_id=2, replica_groups=mesh['tok'=64,'head'=4] {'tok'}, dimensions={1}, use_global_device_ids=true | all-gather | bytes 532480 | tf_op jit(solution)/shard_map/all_gather | solution.py:149
  62.1 49.5 %all-gather.2 = bf16[1,512,512]{2,1,0:T(8,128)(2,1)S(1)} all-gather(bf16[1,8,512]{2,1,0:T(8,128)(2,1)S(1)} %copy-done.104), channel_id=4, replica_groups=mesh['tok'=64,'head'=4] {'tok'}, dimensions={1}, use_global_device_ids=true | all-gather | bytes 532480 | tf_op jit(solution)/shard_map/all_gather | solution.py:151
  111.6 48.1 %all-gather.1 = bf16[1,512,512]{2,1,0:T(8,128)(2,1)S(1)} all-gather(bf16[1,8,512]{2,1,0:T(8,128)(2,1)S(1)} %copy-done.105), channel_id=3, replica_groups=mesh['tok'=64,'head'=4] {'tok'}, dimensions={1}, use_global_device_ids=true | all-gather | bytes 532480 | tf_op jit(solution)/shard_map/all_gather | solution.py:150
  171.2 185.0 %all-reduce.8.cloned.1.call-done = (f32[512,512]{0,1:T(8,128)}, f32[512,512]{0,1:T(8,128)}, f32[512,512]{0,1:T(8,128)}) async-done(((f32[512,512]{0,1:T(8,128)}, f32[512,512]{0,1:T(8,128)}, f32[512,512]{0,1:T(8,128)}), (f32[512,512]{0,1:T(8,128)}, f32[512,512]{0,1:T(8,128)}, f32[512,512]{0,1:T(8,128)})) %all-reduce.8.cloned.1.call-update) | async-done | bytes 3145744 | tf_op jit(solution)/shard_map/psum | solution.py:158
  356.2 2.2 multiply_reduce_fusion.2
  384.3 1.5 fusion.129
  385.8 9.1 all-reduce.2
  395.5 2.0 fusion.128
  402.1 2.1 multiply_convert_fusion.6
  406.1 188.3 %all-reduce.6.cloned.1.call-done = (f32[512,512]{0,1:T(8,128)}, f32[512,512]{0,1:T(8,128)}, f32[512,512]{0,1:T(8,128)}) async-done(((f32[512,512]{0,1:T(8,128)}, f32[512,512]{0,1:T(8,128)}, f32[512,512]{0,1:T(8,128)}), (f32[512,512]{0,1:T(8,128)}, f32[512,512]{0,1:T(8,128)}, f32[512,512]{0,1:T(8,128)})) %all-reduce.6.cloned.1.call-update) | async-done | bytes 3145744 | tf_op jit(solution)/shard_map/psum | solution.py:177
  594.4 3.3 convolution_add_fusion.13
  597.7 1.5 fusion.131
  599.1 2.6 copy.72
  601.7 1.8 fusion.75
  605.7 2.6 copy.73
  608.2 2.7 fusion.30
  611.0 1.5 convolution_add_fusion.11
  612.5 1.5 fusion.169
  613.9 1.5 convolution_add_fusion.9
  615.4 1.4 fusion.132
  616.9 2.6 copy.80
  619.4 1.8 fusion.67
  623.4 2.6 copy.81
  626.0 2.7 fusion.32
  631.6 1.5 convolution_add_fusion.5
  633.1 1.4 fusion.133
  634.6 2.6 copy.91
  637.1 1.8 fusion.59
  641.1 2.6 copy.92
  643.7 2.7 fusion.34
  646.4 1.5 convolution_add_fusion.3
  648.0 1.5 fusion.177
  649.4 2.5 copy.76
  652.0 1.8 fusion.71
  656.0 2.5 copy.77
  658.5 2.6 copy.84
  661.1 1.8 fusion.63
  665.1 2.6 copy.85
  667.6 4.1 fusion.45
  672.4 4.4 fusion.48
  677.4 2.9 fusion.44
  682.2 2.6 copy.95
  688.8 3.8 fusion.51
  698.8 2.5 copy.128
  703.9 2.5 copy.130
  720.1 116.6 %reduce-scatter.10.cloned.1.call-done = f32[8,512]{1,0:T(8,128)} async-done(((f32[512,512]{1,0:T(8,128)}), f32[8,512]{1,0:T(8,128)}) %reduce-scatter.10.cloned.1.call-update) | async-done | bytes 16400
  839.3 139.7 %reduce-scatter.12.cloned.1.call-done = f32[8,512]{1,0:T(8,128)} async-done(((f32[512,512]{1,0:T(8,128)}), f32[8,512]{1,0:T(8,128)}) %reduce-scatter.12.cloned.1.call-update) | async-done | bytes 16400
  981.7 139.7 %reduce-scatter.14.cloned.1.call-done = f32[8,512]{1,0:T(8,128)} async-done(((f32[512,512]{1,0:T(8,128)}), f32[8,512]{1,0:T(8,128)}) %reduce-scatter.14.cloned.1.call-update) | async-done | bytes 16400
  (313 shorter events, 91.3 us)
Async XLA Ops:
  7.2 152.5 %copy-start = (bf16[128,512]{1,0:T(8,128)(2,1)S(1)}, bf16[128,512]{1,0:T(8,128)(2,1)}, u32[]{:S(2)}) copy-start(bf16[128,512]{1,0:T(8,128)(2,1)} %param.9) | copy-start | bytes 393220
  7.2 54.9 %copy-start.104 = (bf16[1,8,512]{2,1,0:T(8,128)(2,1)S(1)}, bf16[1,8,512]{2,1,0:T(8,128)(2,1)}, u32[]{:S(2)}) copy-start(bf16[1,8,512]{2,1,0:T(8,128)(2,1)} %param.15) | copy-start | bytes 24580
  7.2 349.0 %all-reduce.8.cloned.1.call-start = ((), (), s32[]{:S(2)}) async-start(), calls=%async_computation.7 | async-start | bytes 6291456 | tf_op jit(solution)/shard_map/psum | solution.py:158
  62.1 49.5 %copy-start.105 = (bf16[1,8,512]{2,1,0:T(8,128)(2,1)S(1)}, bf16[1,8,512]{2,1,0:T(8,128)(2,1)}, u32[]{:S(2)}) copy-start(bf16[1,8,512]{2,1,0:T(8,128)(2,1)} %param.14) | copy-start | bytes 24580
  159.7 10.5 copy-start.5
  162.4 1.4 copy-start.46
  162.4 2.7 copy-start.48
  166.4 428.0 %all-reduce.6.cloned.1.call-start = ((), (), s32[]{:S(2)}) async-start(), calls=%async_computation.6 | async-start | bytes 6291456 | tf_op jit(solution)/shard_map/psum | solution.py:177
  356.2 2.9 copy-start.2
  361.3 1.7 copy-start.31
  363.6 2.6 copy-start.3
  367.9 1.7 copy-start.20
  371.8 1.5 copy-start.1
  375.0 1.8 copy-start.16
  377.6 4.8 copy-start.26
  380.2 2.1 copy-start.41
  383.1 2.6 copy-start.60
  383.6 2.1 copy-start.40
  395.5 2.0 copy-start.59
  401.8 434.9 %reduce-scatter.10.cloned.1.call-start = ((), (), s32[]{:S(2)}) async-start(), calls=%async_computation.3 | async-start | bytes 1064960
  594.4 3.3 copy-start.9
  594.4 3.3 copy-start.32
  601.7 2.6 copy-start.84
  608.2 2.7 copy-start.80
  611.0 1.5 copy-start.19
  612.5 1.5 copy-start.8
  612.5 1.5 copy-start.44
  613.9 1.5 copy-start.30
  619.4 2.6 copy-start.82
  626.0 2.7 copy-start.76
  628.7 1.4 copy-start.21
  630.2 1.4 copy-start.7
  630.2 1.4 copy-start.42
  631.6 1.5 copy-start.27
  637.1 2.6 copy-start.78
  643.7 2.7 copy-start.74
  646.4 1.5 copy-start.17
  652.0 2.6 copy-start.70
  661.1 2.5 copy-start.72
  682.2 2.6 copy-start.4
  684.8 2.2 copy-start.68
  693.3 1.6 copy-start.96
  693.3 1.6 copy-start.100
  693.3 1.6 copy-start.108
  695.7 1.8 copy-start.24
  696.9 5.7 copy-start.91
  701.4 277.7 %reduce-scatter.12.cloned.1.call-start = ((), (), s32[]{:S(2)}) async-start(), calls=%async_computation.4 | async-start | bytes 1064960
  706.4 415.0 %reduce-scatter.14.cloned.1.call-start = ((), (), s32[]{:S(2)}) async-start(), calls=%async_computation.5 | async-start | bytes 1064960
  (67 other events, 65.9 us)
Sparse Core Ops, SparseCore 0:
  166.5 189.6 all-reduce.7
  401.9 192.3 all-reduce.5
  701.5 135.1 reduce-scatter.9
  840.5 138.5 reduce-scatter.11
  982.9 138.5 reduce-scatter.13
where the time goes:
time: 1140 us; the launch traced here: 1130 us
  waiting for transfers between devices  769 us (67%)
  blocking collectives  162 us (14%)
  matrix products  85.5 us (8%)
  local copies, waits for them, and re-layouts  69.9 us (6%)
  other arithmetic  24.7 us (2%)
  between operations  19 us (2%)
    unnamed x8, waiting for transfers between devices  396 us
    psum x1, waiting for transfers between devices, per_device(): lax.psum((partial_second[0], partial_second[1], partial_second[2]), 'tok')  188 us
    psum x1, waiting for transfers between devices, per_device(): totals = lax.psum((fast[0], fast[1], fast[2]), 'tok')  185 us
    all_gather x1, blocking collectives, per_device(): lax.all_gather(own_rows[0], 'tok', axis=0, tiled=True)  54.9 us
    dot_general x42, matrix products, product(): return jnp.dot(left, right, preferred_element_type=jnp.float32)  54.5 us
    all_gather x1, blocking collectives, per_device(): lax.all_gather(own_rows[2], 'tok', axis=0, tiled=True)  49.5 us
    all_gather x1, blocking collectives, per_device(): lax.all_gather(own_rows[1], 'tok', axis=0, tiled=True)  48.1 us
    unnamed x228, local copies, waits for them, and re-layouts  37.3 us
  transfers between devices with their start and end apart: 5, of which 5 were waited for; matrix products, arithmetic and copies ran while one was open for 2% of the time, Pallas kernels for 0%

commit v1 on v0

v1 whole, which is shorter than its diff:
```python
import math

import jax
import jax.numpy as jnp
from jax import lax
from jax.experimental import pallas as pl
from jax.experimental.pallas import tpu as pltpu
from jax.sharding import PartitionSpec as P

lin_coef = 3.4445
cube_coef = -4.775
fifth_coef = 2.0315
rms_eps = 1e-06
fro_eps = 1e-07

X, Z, HEADS = 4, 8, 4
D = 512
T = 128
HALF = 256
PIECE = 16
ROWS = 128
F32, BF16 = jnp.float32, jnp.bfloat16
MESH = pl.DeviceIdType.MESH


def mm(a, b):
    return jnp.dot(a, b, preferred_element_type=F32)


def mt(a, b):
    return lax.dot_general(a, b, (((1,), (1,)), ((), ())), preferred_element_type=F32)


def sigmoid(v):
    return 1.0 / (1.0 + jnp.exp(-v))


def turned(v):
    return v.astype(F32).T.astype(BF16)


def kernel(
    q_hbm, k_hbm, v_hbm, up_hbm, gain_ref, g_rows, u_rows, d_rows,
    gq_out, gk_out, gv_out, gg_out, gu_out, gd_out,
    q_ref, k_ref, v_ref, up_ref, in_sem,
    wf, wx, w0, gh, pt, w1, a0, b0, x1, a1, b1, cc,
    gk_s, uk_s, back_s, hid_k, hidn_t, rg,
    q1_t, hq1_t, r1, lt, rf,
    oq, gq_s, uq_s, st, sr,
    cs, cr, acc, xs1p, xs1m, xr1l, xr1r, xs2p, xs2m, xr2l, xr2r, xblk, zs, zr,
    piece, norms, fx, fr,
    ag_send, ag_recv, rs_send, rs_recv, st_send, st_recv, pair_send, pair_recv,
):
    tok = lax.axis_index("tok")
    y = lax.axis_index("head")
    c = lax.rem(tok, 2)
    o = 1 - c
    chip = lax.div(tok, 2)
    z = lax.rem(chip, Z)
    x = lax.div(chip, Z)
    xp, xm, x2 = lax.rem(x + 1, X), lax.rem(x + 3, X), lax.rem(x + 2, X)

    def device(x_, z_, c_):
        return ((x_ * Z + z_) * 2 + c_, y)

    partner = device(x, z, o)
    right, left = device(xp, z, c), device(xm, z, c)
    z_to = [device(x, lax.rem(z + step, Z), c) for step in range(1, Z)]
    y_to = [(tok, lax.rem(y + step, HEADS)) for step in range(1, HEADS)]
    mine = pl.ds(pl.multiple_of(c * HALF, HALF), HALF)
    other = pl.ds(pl.multiple_of(o * HALF, HALF), HALF)

    def rows(start, size):
        return pl.ds(pl.multiple_of(start, 16), size)

    loads = [
        pltpu.make_async_copy(source, target, in_sem.at[i])
        for i, (source, target) in enumerate(
            ((k_hbm, k_ref), (v_hbm, v_ref), (q_hbm, q_ref), (up_hbm, up_ref))
        )
    ]
    for load in loads:
        load.start()

    barrier = pltpu.get_barrier_semaphore()
    peers = [partner, right, left] + z_to + y_to
    for peer in peers:
        pl.semaphore_signal(barrier, inc=1, device_id=peer, device_id_type=MESH)
    pl.semaphore_wait(barrier, len(peers))

    sent = []

    def remote(source, target, send, recv, peer):
        return pltpu.make_async_remote_copy(
            src_ref=source, dst_ref=target, send_sem=send, recv_sem=recv,
            device_id=peer, device_id_type=MESH,
        )

    def push(*args):
        copy = remote(*args)
        copy.start()
        sent.append(copy)

    for w, ref in enumerate((g_rows, u_rows, d_rows)):
        wf[w] = ref[0].astype(F32)
    push(
        wf.at[:, :, other], wx.at[:, pl.ds(pl.multiple_of(c * 8, 8), 8), :],
        pair_send.at[0], pair_recv.at[0], partner,
    )
    wx[:, pl.ds(pl.multiple_of(c * 8, 8), 8), :] = wf[:, :, mine]
    remote(
        wf.at[:, :, other], wx.at[:, pl.ds(pl.multiple_of(o * 8, 8), 8), :],
        pair_send.at[0], pair_recv.at[0], partner,
    ).wait_recv()
    w0[:, rows(chip * PIECE, PIECE), mine] = wx[...].astype(BF16)

    def gather(buf, phase):
        def block(w, x_, side, skip=0, size=ROWS):
            return buf.at[w, rows(x_ * ROWS + skip, size), side]

        def go(w, index, ref, peer):
            push(ref, ref, ag_send.at[phase, w, index], ag_recv.at[phase, w, index], peer)

        def come(w, index, ref):
            remote(
                ref, ref, ag_send.at[phase, w, index], ag_recv.at[phase, w, index], partner
            ).wait_recv()

        for w in range(3):
            for step in range(1, Z):
                go(w, step - 1, buf.at[w, rows(chip * PIECE, PIECE), mine], z_to[step - 1])
        yield
        for w in range(3):
            for step in range(1, Z):
                origin = x * ROWS + lax.rem(z + Z - step, Z) * PIECE
                come(w, step - 1, buf.at[w, rows(origin, PIECE), mine])
            go(w, 7, block(w, x, mine), right)
            go(w, 8, block(w, x, mine), left)
            go(w, 11, block(w, x, mine), partner)
        yield
        for w in range(3):
            come(w, 7, block(w, xm, mine))
            go(w, 9, block(w, xm, mine, 0, 64), right)
            come(w, 8, block(w, xp, mine))
            go(w, 10, block(w, xp, mine, 64, 64), left)
            go(w, 12, block(w, xm, mine), partner)
            go(w, 13, block(w, xp, mine), partner)
        yield
        for w in range(3):
            come(w, 9, block(w, x2, mine, 0, 64))
            come(w, 10, block(w, x2, mine, 64, 64))
            go(w, 14, block(w, x2, mine), partner)
        yield
        for w in range(3):
            for index, x_ in ((11, x), (12, xm), (13, xp), (14, x2)):
                come(w, index, block(w, x_, other))
        yield

    def reduce(partial, phase):
        def go(w, index, source, target, peer):
            push(source, target, rs_send.at[phase, w, index], rs_recv.at[phase, w, index], peer)

        def come(w, index, ref):
            remote(
                ref, ref, rs_send.at[phase, w, index], rs_recv.at[phase, w, index], partner
            ).wait_recv()

        for w in range(3):
            cs[phase, w] = partial(w, other).astype(BF16)
            go(w, 0, cs.at[phase, w], cr.at[phase, w], partner)
        for w in range(3):
            acc[w] = partial(w, mine)
        yield
        for w in range(3):
            come(w, 0, cr.at[phase, w])

            def total(x_, skip, w=w):
                span = rows(x_ * ROWS + skip, 64)
                return acc[w, span, :] + cr[phase, w, span, :].astype(F32)

            xs1p[phase, w, :64] = total(x2, 0).astype(BF16)
            xs1p[phase, w, 64:] = total(xp, 64).astype(BF16)
            go(w, 1, xs1p.at[phase, w], xr1l.at[phase, w], right)
            xs1m[phase, w, :64] = total(xm, 0).astype(BF16)
            xs1m[phase, w, 64:] = total(x2, 64).astype(BF16)
            go(w, 2, xs1m.at[phase, w], xr1r.at[phase, w], left)
        yield
        for w in range(3):

            def total(x_, skip, w=w):
                span = rows(x_ * ROWS + skip, 64)
                return acc[w, span, :] + cr[phase, w, span, :].astype(F32)

            come(w, 1, xr1l.at[phase, w])
            xs2p[phase, w] = (total(xp, 0) + xr1l[phase, w, :64].astype(F32)).astype(BF16)
            go(w, 3, xs2p.at[phase, w], xr2l.at[phase, w], right)
            come(w, 2, xr1r.at[phase, w])
            xs2m[phase, w] = (total(xm, 64) + xr1r[phase, w, 64:].astype(F32)).astype(BF16)
            go(w, 4, xs2m.at[phase, w], xr2r.at[phase, w], left)
            xblk[w, :64] = total(x, 0) + xr1r[phase, w, :64].astype(F32)
            xblk[w, 64:] = total(x, 64) + xr1l[phase, w, 64:].astype(F32)
        yield
        for w in range(3):
            come(w, 3, xr2l.at[phase, w])
            come(w, 4, xr2r.at[phase, w])
            xblk[w, :64] = xblk[w, :64] + xr2l[phase, w].astype(F32)
            xblk[w, 64:] = xblk[w, 64:] + xr2r[phase, w].astype(F32)
            zs[phase, w] = xblk[w].astype(BF16)
            for step in range(1, Z):
                target = lax.rem(z + step, Z)
                go(
                    w, 4 + step, zs.at[phase, w, rows(target * PIECE, PIECE), :],
                    zr.at[phase, w, step - 1], z_to[step - 1],
                )
        yield
        for w in range(3):
            total_piece = xblk[w, rows(z * PIECE, PIECE), :]
            for step in range(1, Z):
                come(w, 4 + step, zr.at[phase, w, step - 1])
                total_piece = total_piece + zr[phase, w, step - 1].astype(F32)
            piece[phase, w] = total_piece
        yield

    def run(steps):
        for _ in steps:
            pass

    run(gather(w0, 0))
    for load in loads:
        load.wait()

    keys, values = k_ref[...], v_ref[...]
    gate_pre, up_pre = mm(keys, w0[0]), mm(keys, w0[1])
    back = -mt(values, w0[2])
    gk_s[...], uk_s[...], back_s[...] = gate_pre, up_pre, back
    sigma = sigmoid(gate_pre)
    active = gate_pre * sigma
    hidden = (active * up_pre).astype(BF16)
    slope = sigma * (1.0 + gate_pre * (1.0 - sigma))
    rg[0] = (back * up_pre * slope).astype(BF16)
    rg[1] = (back * active).astype(BF16)
    rg[2] = values
    hid_k[...] = hidden
    hidn_t[...] = turned(-hidden.astype(F32))
    lt[0, :, T:] = turned(keys)
    rf[2, T:] = values

    def fast_partial(w, side):
        left_t = hidn_t[...] if w == 2 else lt[0, :, T:]
        return mm(left_t, rg[w, :, side])

    def apply_forward(b, weights):
        queries = q_ref[b]
        pre, upper = mm(queries, weights[0]), mm(queries, weights[1])
        sq = sigmoid(pre)
        hidden_q = (pre * sq * upper).astype(BF16)
        output = mm(hidden_q, weights[2])
        gq_s[...], uq_s[...], oq[...] = pre, upper, output
        weighted = gain_ref[...] * up_ref[b].astype(F32)
        power = jnp.sum(output * output, axis=1, keepdims=True)
        dots = jnp.sum(weighted * output, axis=1, keepdims=True)
        lane = lax.broadcasted_iota(jnp.int32, (T, T), 1)
        both = jnp.where(lane == 0, jnp.broadcast_to(power, (T, T)), jnp.broadcast_to(dots, (T, T)))
        st[b] = both.T[:8]
        for step in range(1, HEADS):
            push(
                st.at[b], sr.at[b, step - 1], st_send.at[b, step - 1], st_recv.at[b, step - 1],
                y_to[step - 1],
            )
        return hidden_q

    def apply_backward(b, weights, right_refs):
        total = st[b]
        for step in range(1, HEADS):
            remote(
                st.at[b], sr.at[b, step - 1], st_send.at[b, step - 1], st_recv.at[b, step - 1],
                y_to[step - 1],
            ).wait_recv()
            total = total + sr[b, step - 1]
        mean = total * (1.0 / (HEADS * D))
        inverse = lax.rsqrt(mean[0:1] + rms_eps)
        ratio = inverse * inverse * inverse * mean[1:2]
        down = jnp.where(
            lax.broadcasted_iota(jnp.int32, (T, T), 0) == 0,
            jnp.broadcast_to(inverse, (T, T)),
            jnp.broadcast_to(ratio, (T, T)),
        ).T
        weighted = gain_ref[...] * up_ref[b].astype(F32)
        d_output = (down[:, 0:1] * weighted - oq[...] * down[:, 1:2]).astype(BF16)
        back_q = mt(d_output, weights[2])
        pre, upper = gq_s[...], uq_s[...]
        sq = sigmoid(pre)
        right_refs[0][...] = (back_q * upper * (sq * (1.0 + pre * (1.0 - sq)))).astype(BF16)
        right_refs[1][...] = (back_q * pre * sq).astype(BF16)
        right_refs[2][...] = d_output

    def query_grad(b, weights, right_refs):
        gq_out[b] = (
            mt(right_refs[0][...], weights[0]) + mt(right_refs[1][...], weights[1])
        ).astype(BF16)

    steps = reduce(fast_partial, 0)
    next(steps)
    hidden_q = apply_forward(0, w0)
    lt[0, :, :T] = turned(q_ref[0])
    lt[1, :, :T] = turned(hidden_q)
    next(steps)
    first_refs = [rf.at[w, pl.ds(0, T), :] for w in range(3)]
    apply_backward(0, w0, first_refs)
    next(steps)
    query_grad(0, w0, first_refs)
    q1_t[...] = turned(q_ref[1])
    next(steps)
    next(steps)
    gh[:, rows(chip * PIECE, PIECE), mine] = piece[0].astype(BF16)
    run(gather(gh, 1))

    def schulz(w, carry):
        fast = gh[w]
        fast32 = fast.astype(F32)
        power = jnp.sum(jnp.sum(fast32 * fast32, axis=1, keepdims=True), axis=0, keepdims=True)
        root = jnp.sqrt(power)
        norm = root + fro_eps
        inv = 1.0 / norm
        norms[w, 0:8] = jnp.broadcast_to(root, (8, 128))
        norms[w, 8:16] = jnp.broadcast_to(norm, (8, 128))
        gram = (mt(fast, fast) * (inv * inv)).astype(BF16)
        a0[w] = gram
        blend = (cube_coef * gram.astype(F32) + fifth_coef * mm(gram, gram)).astype(BF16)
        b0[w] = blend
        iterate = (inv * (lin_coef * gh[w].astype(F32) + mm(blend, gh[w]))).astype(BF16)
        x1[w] = iterate
        gram = mt(iterate, iterate).astype(BF16)
        a1[w] = gram
        blend = (cube_coef * gram.astype(F32) + fifth_coef * mm(gram, gram)).astype(BF16)
        b1[w] = blend
        final = (lin_coef * x1[w].astype(F32) + mm(blend, x1[w])).astype(BF16)
        w1[w] = (w0[w].astype(F32) - final.astype(F32)).astype(BF16)
        return carry

    lax.fori_loop(0, 3, schulz, 0)

    hidden_q = apply_forward(1, w1)
    hq1_t[...] = turned(hidden_q)
    second_refs = [r1.at[w] for w in range(3)]
    apply_backward(1, w1, second_refs)

    def second_partial(w, side):
        left_t = hq1_t[...] if w == 2 else q1_t[...]
        return mm(left_t, r1[w, :, side])

    steps = reduce(second_partial, 1)
    next(steps)
    query_grad(1, w1, second_refs)
    run(steps)
    pt[:, rows(chip * PIECE, PIECE), mine] = (-piece[1]).astype(BF16)
    run(gather(pt, 2))

    def schulz_back(w, carry):
        root, norm = norms[w, 0:1, 0:1], norms[w, 8:9, 0:1]
        inv = 1.0 / norm

        def sweep(current, iterate, gram, blend, scale):
            cross = mt(current, iterate) + mt(iterate, current)
            if scale is not None:
                cross = cross * scale
            symmetric = cross.astype(BF16)
            bent = mm(symmetric, gram) + mm(gram, symmetric)
            mixed = (cube_coef * symmetric.astype(F32) + fifth_coef * bent).astype(BF16)
            follow = mm(mixed, iterate)
            if scale is not None:
                follow = follow * scale
            return (lin_coef * current.astype(F32) + mm(blend, current) + follow).astype(BF16)

        current = sweep(pt[w], x1[w], a1[w], b1[w], None)
        bottom = sweep(current, gh[w], a0[w], b0[w], inv).astype(F32)
        fast = gh[w].astype(F32)
        inner = jnp.sum(jnp.sum(bottom * fast, axis=1, keepdims=True), axis=0, keepdims=True)
        cc[w] = (bottom * inv - fast * (inner / (norm * norm * root))).astype(BF16)
        return carry

    lax.fori_loop(0, 3, schulz_back, 0)

    keys, values = k_ref[...], v_ref[...]
    along_gate, along_up = mm(keys, cc[0]), mm(keys, cc[1])
    along_hidden = -mt(values, cc[2])
    gate_pre, up_pre, back = gk_s[...], uk_s[...], back_s[...]
    sigma = sigmoid(gate_pre)
    active = gate_pre * sigma
    slope = sigma * (1.0 + gate_pre * (1.0 - sigma))
    curve = sigma * (1.0 - sigma) * (2.0 + gate_pre * (1.0 - 2.0 * sigma))
    d_back = (along_gate * up_pre * slope + along_up * active).astype(BF16)
    rf[1, T:] = (along_gate * back * slope + along_hidden * active).astype(BF16)
    rf[0, T:] = (
        along_gate * back * up_pre * curve + along_up * back * slope + along_hidden * up_pre * slope
    ).astype(BF16)
    lt[1, :, T:] = turned(-d_back.astype(F32))
    r1[2] = d_back

    def last_partial(w, side):
        return mm(lt[w // 2], rf[w, :, side])

    steps = reduce(last_partial, 2)
    next(steps)
    gk_out[...] = (
        mt(rg[0], cc[0]) + mt(rg[1], cc[1]) + mt(rf[0, T:], w0[0]) + mt(rf[1, T:], w0[1])
    ).astype(BF16)
    next(steps)
    gv_out[...] = (-mm(hid_k[...], cc[2]) - mm(r1[2], w0[2])).astype(BF16)
    run(steps)

    scale = 1.0 / math.sqrt(8192)
    fx[...] = (piece[1] + piece[2]) * scale
    push(
        fx.at[:, pl.ds(pl.multiple_of(o * 8, 8), 8), :], fr.at[:, :, mine],
        pair_send.at[1], pair_recv.at[1], partner,
    )
    fr[:, :, mine] = fx[:, pl.ds(pl.multiple_of(c * 8, 8), 8), :]
    remote(
        fx.at[:, pl.ds(pl.multiple_of(o * 8, 8), 8), :], fr.at[:, :, other],
        pair_send.at[1], pair_recv.at[1], partner,
    ).wait_recv()
    for w, out in enumerate((gg_out, gu_out, gd_out)):
        out[0] = fr[w]
    for copy in sent:
        copy.wait_send()


def per_device(queries, keys, values, upstream, out_gain, gate_weight, up_weight, down_weight):
    vmem = pl.BlockSpec(memory_space=pltpu.VMEM)
    hbm = pl.BlockSpec(memory_space=pl.ANY)
    square = pltpu.VMEM((3, D, D), BF16)
    wide = pltpu.VMEM((T, D), F32)
    dma = pltpu.SemaphoreType.DMA
    scratch = [
        pltpu.VMEM((2, T, D), BF16), pltpu.VMEM((T, D), BF16), pltpu.VMEM((T, D), BF16),
        pltpu.VMEM((2, T, D), BF16), dma((4,)),
        pltpu.VMEM((3, 8, D), F32), pltpu.VMEM((3, PIECE, HALF), F32),
    ] + [square] * 10 + [
        wide, wide, wide, pltpu.VMEM((T, D), BF16), pltpu.VMEM((D, T), BF16),
        pltpu.VMEM((3, T, D), BF16),
        pltpu.VMEM((D, T), BF16), pltpu.VMEM((D, T), BF16), pltpu.VMEM((3, T, D), BF16),
        pltpu.VMEM((2, D, 2 * T), BF16), pltpu.VMEM((3, 2 * T, D), BF16),
        wide, wide, wide, pltpu.VMEM((2, 8, 128), F32), pltpu.VMEM((2, 3, 8, 128), F32),
        pltpu.VMEM((3, 3, D, HALF), BF16), pltpu.VMEM((3, 3, D, HALF), BF16),
        pltpu.VMEM((3, D, HALF), F32),
    ] + [pltpu.VMEM((3, 3, 128, HALF), BF16)] * 4 + [pltpu.VMEM((3, 3, 64, HALF), BF16)] * 4 + [
        pltpu.VMEM((3, 128, HALF), F32), pltpu.VMEM((3, 3, 128, HALF), BF16),
        pltpu.VMEM((3, 3, Z - 1, PIECE, HALF), BF16),
        pltpu.VMEM((3, 3, PIECE, HALF), F32), pltpu.VMEM((3, 16, 128), F32),
        pltpu.VMEM((3, PIECE, HALF), F32), pltpu.VMEM((3, 8, D), F32),
        dma((3, 3, 15)), dma((3, 3, 15)), dma((3, 3, 12)), dma((3, 3, 12)),
        dma((2, 3)), dma((2, 3)), dma((2,)), dma((2,)),
    ]
    grad = jax.ShapeDtypeStruct((1, 8, D), F32)
    return pl.pallas_call(
        kernel,
        out_shape=(
            jax.ShapeDtypeStruct((2, T, D), BF16), jax.ShapeDtypeStruct((T, D), BF16),
            jax.ShapeDtypeStruct((T, D), BF16), grad, grad, grad,
        ),
        in_specs=[hbm] * 4 + [vmem] * 4,
        out_specs=[vmem] * 6,
        scratch_shapes=scratch,
        compiler_params=pltpu.CompilerParams(
            collective_id=0, has_side_effects=True, vmem_limit_bytes=60 * 1024 * 1024
        ),
    )(queries, keys, values, upstream, out_gain[None], gate_weight, up_weight, down_weight)


def solution(mesh):
    in_specs = (
        P(None, "tok", "head"),
        P("tok", "head"),
        P("tok", "head"),
        P(None, "tok", "head"),
        P("head"),
        P("head", "tok", None),
        P("head", "tok", None),
        P("head", "tok", None),
    )
    out_specs = (
        P(None, "tok", "head"),
        P("tok", "head"),
        P("tok", "head"),
        P("head", "tok", None),
        P("head", "tok", None),
        P("head", "tok", None),
    )
    return jax.shard_map(
        per_device, mesh=mesh, in_specs=in_specs, out_specs=out_specs, check_vma=False
    )
```

time: 1140 us -> 150 us (0.13)
  waiting for transfers between devices: 769 us -> 0 us
  blocking collectives: 162 us -> 0 us
  Pallas kernels: 0 us -> 143 us
  matrix products: 85.5 us -> 0 us
  local copies, waits for them, and re-layouts: 69.9 us -> 5.43 us
  other arithmetic: 24.7 us -> 0 us
  between operations: 19 us -> 0.66 us
    unnamed x8 -> x0, waiting for transfers between devices: 396 us -> none
    psum x2 -> x0, waiting for transfers between devices: 373 us -> none  [the longest x1 188 us: per_device(): lax.psum((partial_second[0], partial_second[1], partial_second[2]), 'tok')]
    all_gather x3 -> x0, blocking collectives: 152 us -> none  [the longest x1 54.9 us: per_device(): lax.all_gather(own_rows[0], 'tok', axis=0, tiled=True)]
    pallas_call x0 -> x1, Pallas kernels: none -> 143 us  [per_device(): pl.pallas_call(kernel, out_shape=(jax.ShapeDtypeStruct((2, T, D), BF16),...]
    dot_general x78 -> x0, matrix products: 85.5 us -> none  [the longest x42 54.5 us: product(): return jnp.dot(left, right, preferred_element_type=jnp.float32)]
    unnamed x228 -> x16, local copies, waits for them, and re-layouts: 37.3 us -> 5.43 us
    dot_general x12 -> x0, local copies, waits for them, and re-layouts: 29.6 us -> none  [the longest x6 15.4 us: against(): lax.dot_general(left, right, (((1,), (1,)), ((), ())), preferred_element_...]
    convert_element_type x12 -> x0, other arithmetic: 16.8 us -> none  [the longest x6 10.2 us: schulz_backward(): symmetric = (cross + cross.T).astype(jnp.bfloat16)]
  transfers between devices with their start and end apart: 5 -> 0, of which waited for: 5 -> 0; matrix products, arithmetic and copies ran while one was open for 2% -> 0% of each run, Pallas kernels for 0% -> 0%
where the time goes in v1:
time: 150 us; the launch traced here: 149 us
  Pallas kernels  143 us (95%)
  local copies, waits for them, and re-layouts  5.43 us (4%)
    pallas_call x1, Pallas kernels, per_device(): pl.pallas_call(kernel, out_shape=(jax.ShapeDtypeStruct((2, T, D), BF16),...  143 us
    unnamed x16, local copies, waits for them, and re-layouts  5.43 us

profile of v1, /device:TPU:1, one launch (start us, length us, event | category | flops | bytes accessed | tf_op | source)
XLA Modules:
  0.0 149.3 jit_solution(16781111845146344328)
XLA Ops:
  0.6 143.2 %shard_map.127 = (bf16[2,128,512]{2,1,0:T(8,128)(2,1)}, bf16[128,512]{1,0:T(8,128)(2,1)}, bf16[128,512]{1,0:T(8,128)(2,1)}, f32[1,8,512]{2,1,0:T(8,128)}, f32[1,8,512]{2,1,0:T(8,128)}, /*index=5*/f32[1,8,512]{2,1,0:T(8,128)}) custom-call(bf16[2,128,512]{2,1,0:T(8,128)(2,1)} %q_hbm.1, bf16[128,512]{1,0:T(8,128)(2,1)} %k_hbm.1, bf16[128,512]{1,0:T(8,128)(2,1)} %v_hbm.1, ...), custom_call_target="tpu_custom_call" | custom-call | tf_op jit(solution)/shard_map/pallas_call | solution.py:456
  143.8 0.0 copy-start.1
  143.8 1.7 %copy.20 = bf16[2,128,512]{2,1,0:T(8,128)(2,1)} copy(bf16[2,128,512]{2,1,0:T(8,128)(2,1)} %get-tuple-element.12) | data formatting | bytes 524288
  145.5 0.0 copy-done.1
  145.5 0.0 copy-start
  145.6 0.7 copy.21
  146.2 0.3 copy-done
  146.5 0.0 copy-start.4
  146.5 0.7 copy.22
  147.2 0.1 copy-done.4
  147.2 0.0 copy-start.3
  147.2 0.6 copy.23
  147.8 0.1 copy-done.3
  147.9 0.0 copy-start.2
  147.9 0.6 copy.24
  148.6 0.1 copy-done.2
  148.7 0.6 copy.25
Async XLA Ops:
  143.8 1.7 %copy-start.1 = (bf16[128,512]{1,0:T(8,128)(2,1)S(1)}, bf16[128,512]{1,0:T(8,128)(2,1)}, u32[]{:S(2)}) copy-start(bf16[128,512]{1,0:T(8,128)(2,1)} %get-tuple-element.13) | copy-start | bytes 393220
  145.5 1.0 copy-start
  146.5 0.7 copy-start.4
  147.2 0.7 copy-start.3
  147.9 0.7 copy-start.2

commit v2 on v1

--- a/solution.py
+++ b/solution.py
@@ -47,9 +47,9 @@
     gk_s, uk_s, back_s, hid_k, hidn_t, rg,
     q1_t, hq1_t, r1, lt, rf,
     oq, gq_s, uq_s, st, sr,
-    cs, cr, acc, xs1p, xs1m, xr1l, xr1r, xs2p, xs2m, xr2l, xr2r, xblk, zs, zr,
+    cs, cr, acc, s1, q1, s2, q2, sx, qx, sz, qz, xblk,
     piece, norms, fx, fr,
-    ag_send, ag_recv, rs_send, rs_recv, st_send, st_recv, pair_send, pair_recv,
+    ag_send, ag_recv, rs_send, rs_recv, ar_send, ar_recv, st_send, st_recv, pair_send, pair_recv,
 ):
     tok = lax.axis_index("tok")
     y = lax.axis_index("head")
@@ -58,14 +58,18 @@
     chip = lax.div(tok, 2)
     z = lax.rem(chip, Z)
     x = lax.div(chip, Z)
-    xp, xm, x2 = lax.rem(x + 1, X), lax.rem(x + 3, X), lax.rem(x + 2, X)
 
     def device(x_, z_, c_):
         return ((x_ * Z + z_) * 2 + c_, y)
 
     partner = device(x, z, o)
-    right, left = device(xp, z, c), device(xm, z, c)
-    z_to = [device(x, lax.rem(z + step, Z), c) for step in range(1, Z)]
+
+    def x_by(step):
+        return device(lax.rem(x + step, X), z, c)
+
+    def z_by(step):
+        return device(x, lax.rem(z + step + Z, Z), c)
+
     y_to = [(tok, lax.rem(y + step, HEADS)) for step in range(1, HEADS)]
     mine = pl.ds(pl.multiple_of(c * HALF, HALF), HALF)
     other = pl.ds(pl.multiple_of(o * HALF, HALF), HALF)
@@ -83,7 +87,7 @@
         load.start()
 
     barrier = pltpu.get_barrier_semaphore()
-    peers = [partner, right, left] + z_to + y_to
+    peers = [partner] + [x_by(step) for step in range(1, X)] + [z_by(step) for step in range(1, Z)] + y_to
     for peer in peers:
         pl.semaphore_signal(barrier, inc=1, device_id=peer, device_id_type=MESH)
     pl.semaphore_wait(barrier, len(peers))
@@ -114,56 +118,106 @@
     ).wait_recv()
     w0[:, rows(chip * PIECE, PIECE), mine] = wx[...].astype(BF16)
 
-    def gather(buf, phase):
-        def block(w, x_, side, skip=0, size=ROWS):
-            return buf.at[w, rows(x_ * ROWS + skip, size), side]
-
-        def go(w, index, ref, peer):
-            push(ref, ref, ag_send.at[phase, w, index], ag_recv.at[phase, w, index], peer)
+    def part(buf, x_, z_, side):
+        return buf.at[:, rows((x_ * Z + lax.rem(z_ + Z, Z)) * PIECE, PIECE), side]
+
+    def gather(buf):
+        def go(index, ref, peer):
+            push(ref, ref, ag_send.at[index], ag_recv.at[index], peer)
+
+        def come(index, ref):
+            remote(ref, ref, ag_send.at[index], ag_recv.at[index], partner).wait_recv()
+
+        def block(x_, side):
+            return buf.at[:, rows(x_ * ROWS, ROWS), side]
+
+        offsets = (0, -1, 1, -2, 2, -3, 3, 4)
+
+        def across(g):
+            ref = part(buf, x, z + offsets[g], mine)
+            for step in (1, 3, 2):
+                go(6 + 3 * g + step, ref, x_by(step))
+
+        own = part(buf, x, z, mine)
+        for g in range(1, Z):
+            go(g - 1, own, z_by(-offsets[g]))
+        across(0)
+        yield
+        for g in range(1, Z):
+            come(g - 1, part(buf, x, z + offsets[g], mine))
+            across(g)
+        go(31, block(x, mine), partner)
+        yield
+        for step in (1, 3, 2):
+            x_ = lax.rem(x + X - step, X)
+            for g in range(Z):
+                come(6 + 3 * g + step, part(buf, x_, z + offsets[g], mine))
+            go(31 + step, block(x_, mine), partner)
+        for step in (0, 1, 3, 2):
+            come(31 + step, block(lax.rem(x + X - step, X), other))
+        yield
+
+    def reduce(partial):
+        def go(index, source, target, peer):
+            push(source, target, rs_send.at[index], rs_recv.at[index], peer)
+
+        def come(index, ref):
+            remote(ref, ref, rs_send.at[index], rs_recv.at[index], partner).wait_recv()
+
+        offsets = (4, 3, -3, 2, -2, 1, -1, 0)
+
+        def total(x_, j):
+            span = rows((x_ * Z + lax.rem(z + offsets[j] + Z, Z)) * PIECE, PIECE)
+            return acc[:, span, :] + cr[2, :, span, :].astype(F32)
+
+        def first(j):
+            for step in (2, 1, 3):
+                s1[j, step - 1] = total(lax.rem(x + step, X), j).astype(BF16)
+                go(2 + 3 * j + step, s1.at[j, step - 1], q1.at[j, step - 1], x_by(step))
+
+        def second(j):
+            result = total(x, j)
+            for step in (1, 3, 2):
+                come(2 + 3 * j + step, q1.at[j, step - 1])
+                result = result + q1[j, step - 1].astype(F32)
+            if j < Z - 1:
+                s2[j] = result.astype(BF16)
+                go(27 + j, s2.at[j], q2.at[j], z_by(offsets[j]))
+            else:
+                fx[...] = result
+
+        for w in range(3):
+            cs[2, w] = partial(w, other).astype(BF16)
+            go(w, cs.at[2, w], cr.at[2, w], partner)
+        for w in range(3):
+            acc[w] = partial(w, mine)
+        yield
+        for w in range(3):
+            come(w, cr.at[2, w])
+        for j in range(Z):
+            first(j)
+        yield
+        for j in range(Z):
+            second(j)
+        result = fx[...]
+        for j in range(Z - 1):
+            come(27 + j, q2.at[j])
+            result = result + q2[j].astype(F32)
+        fx[...] = result
+        yield
+
+    def combine(partial, phase, buf, sign):
+        def go(w, index, source, target, peer):
+            push(source, target, ar_send.at[phase, w, index], ar_recv.at[phase, w, index], peer)
 
         def come(w, index, ref):
-            remote(
-                ref, ref, ag_send.at[phase, w, index], ag_recv.at[phase, w, index], partner
-            ).wait_recv()
-
-        for w in range(3):
-            for step in range(1, Z):
-                go(w, step - 1, buf.at[w, rows(chip * PIECE, PIECE), mine], z_to[step - 1])
-        yield
-        for w in range(3):
-            for step in range(1, Z):
-                origin = x * ROWS + lax.rem(z + Z - step, Z) * PIECE
-                come(w, step - 1, buf.at[w, rows(origin, PIECE), mine])
-            go(w, 7, block(w, x, mine), right)
-            go(w, 8, block(w, x, mine), left)
-            go(w, 11, block(w, x, mine), partner)
-        yield
-        for w in range(3):
-            come(w, 7, block(w, xm, mine))
-            go(w, 9, block(w, xm, mine, 0, 64), right)
-            come(w, 8, block(w, xp, mine))
-            go(w, 10, block(w, xp, mine, 64, 64), left)
-            go(w, 12, block(w, xm, mine), partner)
-            go(w, 13, block(w, xp, mine), partner)
-        yield
-        for w in range(3):
-            come(w, 9, block(w, x2, mine, 0, 64))
-            come(w, 10, block(w, x2, mine, 64, 64))
-            go(w, 14, block(w, x2, mine), partner)
-        yield
-        for w in range(3):
-            for index, x_ in ((11, x), (12, xm), (13, xp), (14, x2)):
-                come(w, index, block(w, x_, other))
-        yield
-
-    def reduce(partial, phase):
-        def go(w, index, source, target, peer):
-            push(source, target, rs_send.at[phase, w, index], rs_recv.at[phase, w, index], peer)
-
-        def come(w, index, ref):
-            remote(
-                ref, ref, rs_send.at[phase, w, index], rs_recv.at[phase, w, index], partner
-            ).wait_recv()
+            remote(ref, ref, ar_send.at[phase, w, index], ar_recv.at[phase, w, index], partner).wait_recv()
+
+        def block(w, x_, side):
+            return buf.at[w, rows(x_ * ROWS, ROWS), side]
+
+        def own(w, z_):
+            return buf.at[w, rows((x * Z + z_) * PIECE, PIECE), mine]
 
         for w in range(3):
             cs[phase, w] = partial(w, other).astype(BF16)
@@ -173,59 +227,75 @@
         yield
         for w in range(3):
             come(w, 0, cr.at[phase, w])
-
-            def total(x_, skip, w=w):
-                span = rows(x_ * ROWS + skip, 64)
-                return acc[w, span, :] + cr[phase, w, span, :].astype(F32)
-
-            xs1p[phase, w, :64] = total(x2, 0).astype(BF16)
-            xs1p[phase, w, 64:] = total(xp, 64).astype(BF16)
-            go(w, 1, xs1p.at[phase, w], xr1l.at[phase, w], right)
-            xs1m[phase, w, :64] = total(xm, 0).astype(BF16)
-            xs1m[phase, w, 64:] = total(x2, 64).astype(BF16)
-            go(w, 2, xs1m.at[phase, w], xr1r.at[phase, w], left)
-        yield
-        for w in range(3):
-
-            def total(x_, skip, w=w):
-                span = rows(x_ * ROWS + skip, 64)
-                return acc[w, span, :] + cr[phase, w, span, :].astype(F32)
-
-            come(w, 1, xr1l.at[phase, w])
-            xs2p[phase, w] = (total(xp, 0) + xr1l[phase, w, :64].astype(F32)).astype(BF16)
-            go(w, 3, xs2p.at[phase, w], xr2l.at[phase, w], right)
-            come(w, 2, xr1r.at[phase, w])
-            xs2m[phase, w] = (total(xm, 64) + xr1r[phase, w, 64:].astype(F32)).astype(BF16)
-            go(w, 4, xs2m.at[phase, w], xr2r.at[phase, w], left)
-            xblk[w, :64] = total(x, 0) + xr1r[phase, w, :64].astype(F32)
-            xblk[w, 64:] = total(x, 64) + xr1l[phase, w, 64:].astype(F32)
-        yield
-        for w in range(3):
-            come(w, 3, xr2l.at[phase, w])
-            come(w, 4, xr2r.at[phase, w])
-            xblk[w, :64] = xblk[w, :64] + xr2l[phase, w].astype(F32)
-            xblk[w, 64:] = xblk[w, 64:] + xr2r[phase, w].astype(F32)
-            zs[phase, w] = xblk[w].astype(BF16)
-            for step in range(1, Z):
+            for step in (2, 1, 3):
+                span = rows(lax.rem(x + step, X) * ROWS, ROWS)
+                sx[phase, w, step - 1] = (
+                    acc[w, span, :] + cr[phase, w, span, :].astype(F32)
+                ).astype(BF16)
+                go(w, step, sx.at[phase, w, step - 1], qx.at[phase, w, step - 1], x_by(step))
+        yield
+        for w in range(3):
+            span = rows(x * ROWS, ROWS)
+            result = acc[w, span, :] + cr[phase, w, span, :].astype(F32)
+            for step in (1, 3, 2):
+                come(w, step, qx.at[phase, w, step - 1])
+                result = result + qx[phase, w, step - 1].astype(F32)
+            xblk[w] = result
+            sz[phase, w] = result.astype(BF16)
+            for step in (4, 3, 5, 2, 6, 1, 7):
                 target = lax.rem(z + step, Z)
                 go(
-                    w, 4 + step, zs.at[phase, w, rows(target * PIECE, PIECE), :],
-                    zr.at[phase, w, step - 1], z_to[step - 1],
+                    w, 3 + step, sz.at[phase, w, rows(target * PIECE, PIECE), :],
+                    qz.at[phase, w, step - 1], z_by(step),
                 )
         yield
         for w in range(3):
-            total_piece = xblk[w, rows(z * PIECE, PIECE), :]
-            for step in range(1, Z):
-                come(w, 4 + step, zr.at[phase, w, step - 1])
-                total_piece = total_piece + zr[phase, w, step - 1].astype(F32)
-            piece[phase, w] = total_piece
-        yield
+            result = xblk[w, rows(z * PIECE, PIECE), :]
+            for step in (1, 7, 2, 6, 3, 5, 4):
+                come(w, 3 + step, qz.at[phase, w, step - 1])
+                result = result + qz[phase, w, step - 1].astype(F32)
+            piece[phase, w] = result
+            buf[w, rows(chip * PIECE, PIECE), mine] = (sign * result).astype(BF16)
+            for step in (4, 3, 5, 2, 6, 1, 7):
+                go(w, 10 + step, own(w, z), own(w, z), z_by(step))
+        yield
+        for w in range(3):
+            for step in (1, 7, 2, 6, 3, 5, 4):
+                come(w, 10 + step, own(w, lax.rem(z + Z - step, Z)))
+            for step in (2, 1, 3):
+                go(w, 17 + step, block(w, x, mine), block(w, x, mine), x_by(step))
+            go(w, 21, block(w, x, mine), block(w, x, mine), partner)
+        yield
+
+    def finish(w, phase, buf):
+        for step in (1, 3, 2):
+            ref = buf.at[w, rows(lax.rem(x + X - step, X) * ROWS, ROWS), mine]
+            remote(
+                ref, ref, ar_send.at[phase, w, 17 + step], ar_recv.at[phase, w, 17 + step], partner
+            ).wait_recv()
+            remote(
+                ref, ref, ar_send.at[phase, w, 21 + step], ar_recv.at[phase, w, 21 + step], partner
+            ).start()
+
+    def follow(w, phase, buf):
+        for step in (0, 1, 3, 2):
+            ref = buf.at[w, rows(lax.rem(x + X - step, X) * ROWS, ROWS), other]
+            remote(
+                ref, ref, ar_send.at[phase, w, 21 + step], ar_recv.at[phase, w, 21 + step], partner
+            ).wait_recv()
+
+    def leave(w, phase, buf):
+        for step in (1, 3, 2):
+            ref = buf.at[w, rows(lax.rem(x + X - step, X) * ROWS, ROWS), mine]
+            remote(
+                ref, ref, ar_send.at[phase, w, 21 + step], ar_recv.at[phase, w, 21 + step], partner
+            ).wait_send()
 
     def run(steps):
         for _ in steps:
             pass
 
-    run(gather(w0, 0))
+    run(gather(w0))
     for load in loads:
         load.wait()
 
@@ -299,23 +369,22 @@
             mt(right_refs[0][...], weights[0]) + mt(right_refs[1][...], weights[1])
         ).astype(BF16)
 
-    steps = reduce(fast_partial, 0)
+    first_refs = [rf.at[w, pl.ds(0, T), :] for w in range(3)]
+    steps = combine(fast_partial, 0, gh, 1.0)
+    next(steps)
     next(steps)
     hidden_q = apply_forward(0, w0)
+    next(steps)
     lt[0, :, :T] = turned(q_ref[0])
     lt[1, :, :T] = turned(hidden_q)
     next(steps)
-    first_refs = [rf.at[w, pl.ds(0, T), :] for w in range(3)]
     apply_backward(0, w0, first_refs)
     next(steps)
-    query_grad(0, w0, first_refs)
     q1_t[...] = turned(q_ref[1])
-    next(steps)
-    next(steps)
-    gh[:, rows(chip * PIECE, PIECE), mine] = piece[0].astype(BF16)
-    run(gather(gh, 1))
+    finish(0, 0, gh)
 
     def schulz(w, carry):
+        follow(w, 0, gh)
         fast = gh[w]
         fast32 = fast.astype(F32)
         power = jnp.sum(jnp.sum(fast32 * fast32, axis=1, keepdims=True), axis=0, keepdims=True)
@@ -330,7 +399,12 @@
         b0[w] = blend
         iterate = (inv * (lin_coef * gh[w].astype(F32) + mm(blend, gh[w]))).astype(BF16)
         x1[w] = iterate
-        gram = mt(iterate, iterate).astype(BF16)
+
+        @pl.when(w < 2)
+        def _():
+            finish(w + 1, 0, gh)
+
+        gram = mt(x1[w], x1[w]).astype(BF16)
         a1[w] = gram
         blend = (cube_coef * gram.astype(F32) + fifth_coef * mm(gram, gram)).astype(BF16)
         b1[w] = blend
@@ -349,31 +423,42 @@
         left_t = hq1_t[...] if w == 2 else q1_t[...]
         return mm(left_t, r1[w, :, side])
 
-    steps = reduce(second_partial, 1)
+    steps = combine(second_partial, 1, pt, -1.0)
+    next(steps)
     next(steps)
     query_grad(1, w1, second_refs)
-    run(steps)
-    pt[:, rows(chip * PIECE, PIECE), mine] = (-piece[1]).astype(BF16)
-    run(gather(pt, 2))
+    next(steps)
+    query_grad(0, w0, first_refs)
+    for _ in steps:
+        pass
+    finish(0, 1, pt)
 
     def schulz_back(w, carry):
+        follow(w, 1, pt)
         root, norm = norms[w, 0:1, 0:1], norms[w, 8:9, 0:1]
         inv = 1.0 / norm
 
         def sweep(current, iterate, gram, blend, scale):
-            cross = mt(current, iterate) + mt(iterate, current)
+            cross = mt(current, iterate)
+            cross = cross + cross.T
             if scale is not None:
                 cross = cross * scale
             symmetric = cross.astype(BF16)
-            bent = mm(symmetric, gram) + mm(gram, symmetric)
+            bent = mm(symmetric, gram)
+            bent = bent + bent.T
             mixed = (cube_coef * symmetric.astype(F32) + fifth_coef * bent).astype(BF16)
             follow = mm(mixed, iterate)
             if scale is not None:
                 follow = follow * scale
             return (lin_coef * current.astype(F32) + mm(blend, current) + follow).astype(BF16)
 
-        current = sweep(pt[w], x1[w], a1[w], b1[w], None)
-        bottom = sweep(current, gh[w], a0[w], b0[w], inv).astype(F32)
+        cc[w] = sweep(pt[w], x1[w], a1[w], b1[w], None)
+
+        @pl.when(w < 2)
+        def _():
+            finish(w + 1, 1, pt)
+
+        bottom = sweep(cc[w], gh[w], a0[w], b0[w], inv).astype(F32)
         fast = gh[w].astype(F32)
         inner = jnp.sum(jnp.sum(bottom * fast, axis=1, keepdims=True), axis=0, keepdims=True)
         cc[w] = (bottom * inv - fast * (inner / (norm * norm * root))).astype(BF16)
@@ -400,7 +485,7 @@
     def last_partial(w, side):
         return mm(lt[w // 2], rf[w, :, side])
 
-    steps = reduce(last_partial, 2)
+    steps = reduce(last_partial)
     next(steps)
     gk_out[...] = (
         mt(rg[0], cc[0]) + mt(rg[1], cc[1]) + mt(rf[0, T:], w0[0]) + mt(rf[1, T:], w0[1])
@@ -410,7 +495,7 @@
     run(steps)
 
     scale = 1.0 / math.sqrt(8192)
-    fx[...] = (piece[1] + piece[2]) * scale
+    fx[...] = (piece[1] + fx[...]) * scale
     push(
         fx.at[:, pl.ds(pl.multiple_of(o * 8, 8), 8), :], fr.at[:, :, mine],
         pair_send.at[1], pair_recv.at[1], partner,
@@ -424,6 +509,14 @@
         out[0] = fr[w]
     for copy in sent:
         copy.wait_send()
+    for phase, buf in enumerate((gh, pt)):
+        for w in range(3):
+            leave(w, phase, buf)
+
+
+def hand_on(*refs):
+    for source, target in zip(refs[:6], refs[6:]):
+        target[...] = source[...]
 
 
 def per_device(queries, keys, values, upstream, out_gain, gate_weight, up_weight, down_weight):
@@ -444,21 +537,23 @@
         wide, wide, wide, pltpu.VMEM((2, 8, 128), F32), pltpu.VMEM((2, 3, 8, 128), F32),
         pltpu.VMEM((3, 3, D, HALF), BF16), pltpu.VMEM((3, 3, D, HALF), BF16),
         pltpu.VMEM((3, D, HALF), F32),
-    ] + [pltpu.VMEM((3, 3, 128, HALF), BF16)] * 4 + [pltpu.VMEM((3, 3, 64, HALF), BF16)] * 4 + [
-        pltpu.VMEM((3, 128, HALF), F32), pltpu.VMEM((3, 3, 128, HALF), BF16),
-        pltpu.VMEM((3, 3, Z - 1, PIECE, HALF), BF16),
-        pltpu.VMEM((3, 3, PIECE, HALF), F32), pltpu.VMEM((3, 16, 128), F32),
+    ] + [pltpu.VMEM((Z, 3, 3, PIECE, HALF), BF16)] * 2 + [pltpu.VMEM((Z - 1, 3, PIECE, HALF), BF16)] * 2 + [
+        pltpu.VMEM((2, 3, 3, ROWS, HALF), BF16), pltpu.VMEM((2, 3, 3, ROWS, HALF), BF16),
+        pltpu.VMEM((2, 3, ROWS, HALF), BF16), pltpu.VMEM((2, 3, Z - 1, PIECE, HALF), BF16),
+        pltpu.VMEM((3, ROWS, HALF), F32),
+        pltpu.VMEM((2, 3, PIECE, HALF), F32), pltpu.VMEM((3, 16, 128), F32),
         pltpu.VMEM((3, PIECE, HALF), F32), pltpu.VMEM((3, 8, D), F32),
-        dma((3, 3, 15)), dma((3, 3, 15)), dma((3, 3, 12)), dma((3, 3, 12)),
+        dma((35,)), dma((35,)), dma((34,)), dma((34,)), dma((2, 3, 25)), dma((2, 3, 25)),
         dma((2, 3)), dma((2, 3)), dma((2,)), dma((2,)),
     ]
     grad = jax.ShapeDtypeStruct((1, 8, D), F32)
-    return pl.pallas_call(
+    shapes = (
+        jax.ShapeDtypeStruct((2, T, D), BF16), jax.ShapeDtypeStruct((T, D), BF16),
+        jax.ShapeDtypeStruct((T, D), BF16), grad, grad, grad,
+    )
+    outs = pl.pallas_call(
         kernel,
-        out_shape=(
-            jax.ShapeDtypeStruct((2, T, D), BF16), jax.ShapeDtypeStruct((T, D), BF16),
-            jax.ShapeDtypeStruct((T, D), BF16), grad, grad, grad,
-        ),
+        out_shape=shapes,
         in_specs=[hbm] * 4 + [vmem] * 4,
         out_specs=[vmem] * 6,
         scratch_shapes=scratch,
@@ -466,6 +561,9 @@
             collective_id=0, has_side_effects=True, vmem_limit_bytes=60 * 1024 * 1024
         ),
     )(queries, keys, values, upstream, out_gain[None], gate_weight, up_weight, down_weight)
+    return pl.pallas_call(
+        hand_on, out_shape=shapes, in_specs=[vmem] * 6, out_specs=[vmem] * 6,
+    )(*outs)
 
 
 def solution(mesh):

time: 150 us -> 127 us (0.85)
  Pallas kernels: 143 us -> 126 us
  local copies, waits for them, and re-layouts: 5.43 us -> 0 us
    pallas_call x1 -> x2, Pallas kernels: 143 us -> 126 us  [the longest x1 124 us: per_device(): pl.pallas_call(kernel, out_shape=shapes, in_specs=[hbm] * 4 + [vmem] * 4,...]
    unnamed x16 -> x0, local copies, waits for them, and re-layouts: 5.43 us -> none
where the time goes in v2:
time: 127 us
  Pallas kernels  126 us (99%)
    pallas_call x1, Pallas kernels, per_device(): pl.pallas_call(kernel, out_shape=shapes, in_specs=[hbm] * 4 + [vmem] * 4,...  124 us

profile of v2, /device:TPU:1, one launch (start us, length us, event | category | flops | bytes accessed | tf_op | source)
XLA Modules:
  0.0 127.0 jit_solution(4183959139307588309)
XLA Ops:
  0.6 124.5 %shard_map.127 = (bf16[2,128,512]{2,1,0:T(8,128)(2,1)}, bf16[128,512]{1,0:T(8,128)(2,1)}, bf16[128,512]{1,0:T(8,128)(2,1)}, f32[1,8,512]{2,1,0:T(8,128)}, f32[1,8,512]{2,1,0:T(8,128)}, /*index=5*/f32[1,8,512]{2,1,0:T(8,128)}) custom-call(bf16[2,128,512]{2,1,0:T(8,128)(2,1)} %q_hbm.1, bf16[128,512]{1,0:T(8,128)(2,1)} %k_hbm.1, bf16[128,512]{1,0:T(8,128)(2,1)} %v_hbm.1, ...), custom_call_target="tpu_custom_call" | custom-call | tf_op jit(solution)/shard_map/pallas_call | solution.py:554
  125.1 1.9 %shard_map.128 = (bf16[2,128,512]{2,1,0:T(8,128)(2,1)}, bf16[128,512]{1,0:T(8,128)(2,1)}, bf16[128,512]{1,0:T(8,128)(2,1)}, f32[1,8,512]{2,1,0:T(8,128)}, f32[1,8,512]{2,1,0:T(8,128)}, /*index=5*/f32[1,8,512]{2,1,0:T(8,128)}) custom-call(bf16[2,128,512]{2,1,0:T(8,128)(2,1)} %get-tuple-element.12.refs_0_, bf16[128,512]{1,0:T(8,128)(2,1)} %get-tuple-element.13.refs_1_, ...), custom_call_target="tpu_custom_call" | custom-call | tf_op jit(solution)/shard_map/pallas_call | solution.py:564

commit v3 on v2

--- a/solution.py
+++ b/solution.py
@@ -15,6 +15,7 @@
 
 X, Z, HEADS = 4, 8, 4
 D = 512
+BLOCK = 8192
 T = 128
 HALF = 256
 PIECE = 16
@@ -40,17 +41,20 @@
 
 
 def kernel(
-    q_hbm, k_hbm, v_hbm, up_hbm, gain_ref, g_rows, u_rows, d_rows,
+    q_hbm, k_hbm, v_hbm, up_hbm, gain_hbm, g_rows, u_rows, d_rows,
     gq_out, gk_out, gv_out, gg_out, gu_out, gd_out,
-    q_ref, k_ref, v_ref, up_ref, in_sem,
-    wf, wx, w0, gh, pt, w1, a0, b0, x1, a1, b1, cc,
+    q_ref, k_ref, v_ref, up_ref, gain_ref, wr, in_sem,
+    wf, wx, w0, w1, a0, a1, cc, be0, be1, yx0, yx1,
     gk_s, uk_s, back_s, hid_k, hidn_t, rg,
     q1_t, hq1_t, r1, lt, rf,
     oq, gq_s, uq_s, st, sr,
-    cs, cr, acc, s1, q1, s2, q2, sx, qx, sz, qz, xblk,
+    cs, cr, acc, s1, q1, s2, q2, s2f, sx, qx, sz, qz, xblk,
     piece, norms, fx, fr,
     ag_send, ag_recv, rs_send, rs_recv, ar_send, ar_recv, st_send, st_recv, pair_send, pair_recv,
 ):
+    low, high = pl.ds(0, D), pl.ds(D, D)
+    gh, pt, x1 = yx0.at[:, high, :], yx1.at[:, low, :], yx1.at[:, high, :]
+    b0, b1 = be0.at[:, :, low], be1.at[:, :, low]
     tok = lax.axis_index("tok")
     y = lax.axis_index("head")
     c = lax.rem(tok, 2)
@@ -67,8 +71,8 @@
     def x_by(step):
         return device(lax.rem(x + step, X), z, c)
 
-    def z_by(step):
-        return device(x, lax.rem(z + step + Z, Z), c)
+    def z_by(step, core=c):
+        return device(x, lax.rem(z + step + Z, Z), core)
 
     y_to = [(tok, lax.rem(y + step, HEADS)) for step in range(1, HEADS)]
     mine = pl.ds(pl.multiple_of(c * HALF, HALF), HALF)
@@ -80,16 +84,25 @@
     loads = [
         pltpu.make_async_copy(source, target, in_sem.at[i])
         for i, (source, target) in enumerate(
-            ((k_hbm, k_ref), (v_hbm, v_ref), (q_hbm, q_ref), (up_hbm, up_ref))
+            (
+                (g_rows.at[0], wr.at[0]), (u_rows.at[0], wr.at[1]), (d_rows.at[0], wr.at[2]),
+                (k_hbm, k_ref), (v_hbm, v_ref), (q_hbm, q_ref), (up_hbm, up_ref),
+                (gain_hbm, gain_ref),
+            )
         )
     ]
     for load in loads:
         load.start()
 
     barrier = pltpu.get_barrier_semaphore()
-    peers = [partner] + [x_by(step) for step in range(1, X)] + [z_by(step) for step in range(1, Z)] + y_to
+    peers = [partner] + [x_by(step) for step in range(1, X)] + y_to
+    for step in range(1, Z):
+        peers += [z_by(step), z_by(step, o)]
     for peer in peers:
         pl.semaphore_signal(barrier, inc=1, device_id=peer, device_id_type=MESH)
+    for w in range(3):
+        loads[w].wait()
+        wf[w] = wr[w].astype(F32)
     pl.semaphore_wait(barrier, len(peers))
 
     sent = []
@@ -105,8 +118,6 @@
         copy.start()
         sent.append(copy)
 
-    for w, ref in enumerate((g_rows, u_rows, d_rows)):
-        wf[w] = ref[0].astype(F32)
     push(
         wf.at[:, :, other], wx.at[:, pl.ds(pl.multiple_of(c * 8, 8), 8), :],
         pair_send.at[0], pair_recv.at[0], partner,
@@ -181,10 +192,19 @@
                 come(2 + 3 * j + step, q1.at[j, step - 1])
                 result = result + q1[j, step - 1].astype(F32)
             if j < Z - 1:
-                s2[j] = result.astype(BF16)
-                go(27 + j, s2.at[j], q2.at[j], z_by(offsets[j]))
+                s2f[...] = result
+                for index, core in enumerate((c, o)):
+                    rows8 = s2f[:, pl.ds(pl.multiple_of(core * 8, 8), 8), :]
+                    s2[j, index] = jnp.concatenate(
+                        [rows8[:, :, :128], rows8[:, :, 128:]], axis=1
+                    ).astype(BF16)
+                    go(27 + 2 * j + index, s2.at[j, index], q2.at[j, index], z_by(offsets[j], core))
             else:
-                fx[...] = result
+                fx[...] = result + piece[1]
+                push(
+                    fx.at[:, pl.ds(pl.multiple_of(o * 8, 8), 8), :], fr.at[:, :, mine],
+                    pair_send.at[1], pair_recv.at[1], partner,
+                )
 
         for w in range(3):
             cs[2, w] = partial(w, other).astype(BF16)
@@ -199,11 +219,22 @@
         yield
         for j in range(Z):
             second(j)
-        result = fx[...]
+        sides = [fx[:, pl.ds(pl.multiple_of(c * 8, 8), 8), :], None]
         for j in range(Z - 1):
-            come(27 + j, q2.at[j])
-            result = result + q2[j].astype(F32)
-        fx[...] = result
+            for index in range(2):
+                come(27 + 2 * j + index, q2.at[j, index])
+        remote(
+            fx.at[:, pl.ds(pl.multiple_of(o * 8, 8), 8), :], fr.at[:, :, other],
+            pair_send.at[1], pair_recv.at[1], partner,
+        ).wait_recv()
+        sides[1] = fr[:, :, other]
+        for j in range(Z - 1):
+            for index in range(2):
+                packed = q2[j, index].astype(F32)
+                sides[index] = sides[index] + jnp.concatenate([packed[:, :8], packed[:, 8:]], axis=2)
+        scale = 1.0 / math.sqrt(BLOCK)
+        fr[:, :, mine] = sides[0] * scale
+        fr[:, :, other] = sides[1] * scale
         yield
 
     def combine(partial, phase, buf, sign):
@@ -296,7 +327,7 @@
             pass
 
     run(gather(w0))
-    for load in loads:
+    for load in loads[3:]:
         load.wait()
 
     keys, values = k_ref[...], v_ref[...]
@@ -438,27 +469,27 @@
         root, norm = norms[w, 0:1, 0:1], norms[w, 8:9, 0:1]
         inv = 1.0 / norm
 
-        def sweep(current, iterate, gram, blend, scale):
-            cross = mt(current, iterate)
+        def sweep(pair, gram, both, scale):
+            cross = mt(pair[w, low], pair[w, high])
             cross = cross + cross.T
             if scale is not None:
                 cross = cross * scale
             symmetric = cross.astype(BF16)
             bent = mm(symmetric, gram)
             bent = bent + bent.T
-            mixed = (cube_coef * symmetric.astype(F32) + fifth_coef * bent).astype(BF16)
-            follow = mm(mixed, iterate)
+            mixed = cube_coef * symmetric.astype(F32) + fifth_coef * bent
             if scale is not None:
-                follow = follow * scale
-            return (lin_coef * current.astype(F32) + mm(blend, current) + follow).astype(BF16)
-
-        cc[w] = sweep(pt[w], x1[w], a1[w], b1[w], None)
+                mixed = mixed * scale
+            both[w, :, high] = mixed.astype(BF16)
+            return (lin_coef * pair[w, low].astype(F32) + mm(both[w], pair[w])).astype(BF16)
+
+        yx0[w, low] = sweep(yx1, a1[w], be1, None)
 
         @pl.when(w < 2)
         def _():
             finish(w + 1, 1, pt)
 
-        bottom = sweep(cc[w], gh[w], a0[w], b0[w], inv).astype(F32)
+        bottom = sweep(yx0, a0[w], be0, inv).astype(F32)
         fast = gh[w].astype(F32)
         inner = jnp.sum(jnp.sum(bottom * fast, axis=1, keepdims=True), axis=0, keepdims=True)
         cc[w] = (bottom * inv - fast * (inner / (norm * norm * root))).astype(BF16)
@@ -494,17 +525,6 @@
     gv_out[...] = (-mm(hid_k[...], cc[2]) - mm(r1[2], w0[2])).astype(BF16)
     run(steps)
 
-    scale = 1.0 / math.sqrt(8192)
-    fx[...] = (piece[1] + fx[...]) * scale
-    push(
-        fx.at[:, pl.ds(pl.multiple_of(o * 8, 8), 8), :], fr.at[:, :, mine],
-        pair_send.at[1], pair_recv.at[1], partner,
-    )
-    fr[:, :, mine] = fx[:, pl.ds(pl.multiple_of(c * 8, 8), 8), :]
-    remote(
-        fx.at[:, pl.ds(pl.multiple_of(o * 8, 8), 8), :], fr.at[:, :, other],
-        pair_send.at[1], pair_recv.at[1], partner,
-    ).wait_recv()
     for w, out in enumerate((gg_out, gu_out, gd_out)):
         out[0] = fr[w]
     for copy in sent:
@@ -515,8 +535,13 @@
 
 
 def hand_on(*refs):
-    for source, target in zip(refs[:6], refs[6:]):
-        target[...] = source[...]
+    copies = [
+        pltpu.make_async_copy(refs[i], refs[6 + i], refs[12].at[i]) for i in range(6)
+    ]
+    for copy in copies:
+        copy.start()
+    for copy in copies:
+        copy.wait()
 
 
 def per_device(queries, keys, values, upstream, out_gain, gate_weight, up_weight, down_weight):
@@ -527,9 +552,9 @@
     dma = pltpu.SemaphoreType.DMA
     scratch = [
         pltpu.VMEM((2, T, D), BF16), pltpu.VMEM((T, D), BF16), pltpu.VMEM((T, D), BF16),
-        pltpu.VMEM((2, T, D), BF16), dma((4,)),
+        pltpu.VMEM((2, T, D), BF16), pltpu.VMEM((1, D), F32), pltpu.VMEM((3, 8, D), BF16), dma((8,)),
         pltpu.VMEM((3, 8, D), F32), pltpu.VMEM((3, PIECE, HALF), F32),
-    ] + [square] * 10 + [
+    ] + [square] * 5 + [pltpu.VMEM((3, D, 2 * D), BF16)] * 2 + [pltpu.VMEM((3, 2 * D, D), BF16)] * 2 + [
         wide, wide, wide, pltpu.VMEM((T, D), BF16), pltpu.VMEM((D, T), BF16),
         pltpu.VMEM((3, T, D), BF16),
         pltpu.VMEM((D, T), BF16), pltpu.VMEM((D, T), BF16), pltpu.VMEM((3, T, D), BF16),
@@ -537,13 +562,14 @@
         wide, wide, wide, pltpu.VMEM((2, 8, 128), F32), pltpu.VMEM((2, 3, 8, 128), F32),
         pltpu.VMEM((3, 3, D, HALF), BF16), pltpu.VMEM((3, 3, D, HALF), BF16),
         pltpu.VMEM((3, D, HALF), F32),
-    ] + [pltpu.VMEM((Z, 3, 3, PIECE, HALF), BF16)] * 2 + [pltpu.VMEM((Z - 1, 3, PIECE, HALF), BF16)] * 2 + [
+    ] + [pltpu.VMEM((Z, 3, 3, PIECE, HALF), BF16)] * 2 + [pltpu.VMEM((Z - 1, 2, 3, PIECE, 128), BF16)] * 2 + [
+        pltpu.VMEM((3, PIECE, HALF), F32),
         pltpu.VMEM((2, 3, 3, ROWS, HALF), BF16), pltpu.VMEM((2, 3, 3, ROWS, HALF), BF16),
         pltpu.VMEM((2, 3, ROWS, HALF), BF16), pltpu.VMEM((2, 3, Z - 1, PIECE, HALF), BF16),
         pltpu.VMEM((3, ROWS, HALF), F32),
         pltpu.VMEM((2, 3, PIECE, HALF), F32), pltpu.VMEM((3, 16, 128), F32),
         pltpu.VMEM((3, PIECE, HALF), F32), pltpu.VMEM((3, 8, D), F32),
-        dma((35,)), dma((35,)), dma((34,)), dma((34,)), dma((2, 3, 25)), dma((2, 3, 25)),
+        dma((35,)), dma((35,)), dma((41,)), dma((41,)), dma((2, 3, 25)), dma((2, 3, 25)),
         dma((2, 3)), dma((2, 3)), dma((2,)), dma((2,)),
     ]
     grad = jax.ShapeDtypeStruct((1, 8, D), F32)
@@ -553,8 +579,8 @@
     )
     outs = pl.pallas_call(
         kernel,
-        out_shape=shapes,
-        in_specs=[hbm] * 4 + [vmem] * 4,
+        out_shape=tuple(pltpu.VMEM(shape.shape, shape.dtype) for shape in shapes),
+        in_specs=[hbm] * 8,
         out_specs=[vmem] * 6,
         scratch_shapes=scratch,
         compiler_params=pltpu.CompilerParams(
@@ -562,8 +588,9 @@
         ),
     )(queries, keys, values, upstream, out_gain[None], gate_weight, up_weight, down_weight)
     return pl.pallas_call(
-        hand_on, out_shape=shapes, in_specs=[vmem] * 6, out_specs=[vmem] * 6,
-    )(*outs)
+        hand_on, out_shape=shapes, in_specs=[vmem] * 6, out_specs=[hbm] * 6,
+        scratch_shapes=[dma((6,))],
+    )(*[pltpu.with_memory_space_constraint(out, pltpu.VMEM) for out in outs])
 
 
 def solution(mesh):

time: 127 us -> 122 us (0.961)
  Pallas kernels: 126 us -> 121 us
    pallas_call x1, Pallas kernels: 124 us -> 120 us  [per_device(): pl.pallas_call(kernel, out_shape=tuple((pltpu.VMEM(shape.shape, shape.dty...]
where the time goes in v3:
time: 122 us
  Pallas kernels  121 us (99%)
    pallas_call x1, Pallas kernels, per_device(): pl.pallas_call(kernel, out_shape=tuple((pltpu.VMEM(shape.shape, shape.dty...  120 us

profile of v3, /device:TPU:1, one launch (start us, length us, event | category | flops | bytes accessed | tf_op | source)
XLA Modules:
  0.0 122.0 jit_solution(16296219206488717635)
XLA Ops:
  0.6 120.3 %shard_map.127 = (bf16[2,128,512]{2,1,0:T(8,128)(2,1)S(1)}, bf16[128,512]{1,0:T(8,128)(2,1)S(1)}, bf16[128,512]{1,0:T(8,128)(2,1)S(1)}, f32[1,8,512]{2,1,0:T(8,1...) custom-call(bf16[2,128,512]{2,1,0:T(8,128)(2,1)} %q_hbm.1, bf16[128,512]{1,0:T(8,128)(2,1)} %k_hbm.1, ...), custom_call_target="tpu_custom_call" | custom-call | tf_op jit(solution)/shard_map/pallas_call | solution.py:580
  121.0 0.8 shard_map.128

commit v4 on v3

--- a/solution.py
+++ b/solution.py
@@ -44,7 +44,7 @@
     q_hbm, k_hbm, v_hbm, up_hbm, gain_hbm, g_rows, u_rows, d_rows,
     gq_out, gk_out, gv_out, gg_out, gu_out, gd_out,
     q_ref, k_ref, v_ref, up_ref, gain_ref, wr, in_sem,
-    wf, wx, w0, w1, a0, a1, cc, be0, be1, yx0, yx1,
+    wq, w0, w1, a0, a1, cc, be0, be1, yx0, yx1,
     gk_s, uk_s, back_s, hid_k, hidn_t, rg,
     q1_t, hq1_t, r1, lt, rf,
     oq, gq_s, uq_s, st, sr,
@@ -91,18 +91,16 @@
             )
         )
     ]
-    for load in loads:
-        load.start()
-
     barrier = pltpu.get_barrier_semaphore()
     peers = [partner] + [x_by(step) for step in range(1, X)] + y_to
     for step in range(1, Z):
         peers += [z_by(step), z_by(step, o)]
     for peer in peers:
         pl.semaphore_signal(barrier, inc=1, device_id=peer, device_id_type=MESH)
+    for load in loads:
+        load.start()
     for w in range(3):
         loads[w].wait()
-        wf[w] = wr[w].astype(F32)
     pl.semaphore_wait(barrier, len(peers))
 
     sent = []
@@ -113,60 +111,55 @@
             device_id=peer, device_id_type=MESH,
         )
 
+    def drain(count):
+        for copy in sent[:count]:
+            copy.wait_send()
+        del sent[:count]
+
     def push(*args):
         copy = remote(*args)
         copy.start()
         sent.append(copy)
 
-    push(
-        wf.at[:, :, other], wx.at[:, pl.ds(pl.multiple_of(c * 8, 8), 8), :],
-        pair_send.at[0], pair_recv.at[0], partner,
-    )
-    wx[:, pl.ds(pl.multiple_of(c * 8, 8), 8), :] = wf[:, :, mine]
-    remote(
-        wf.at[:, :, other], wx.at[:, pl.ds(pl.multiple_of(o * 8, 8), 8), :],
-        pair_send.at[0], pair_recv.at[0], partner,
-    ).wait_recv()
-    w0[:, rows(chip * PIECE, PIECE), mine] = wx[...].astype(BF16)
-
-    def part(buf, x_, z_, side):
-        return buf.at[:, rows((x_ * Z + lax.rem(z_ + Z, Z)) * PIECE, PIECE), side]
-
-    def gather(buf):
-        def go(index, ref, peer):
-            push(ref, ref, ag_send.at[index], ag_recv.at[index], peer)
+    def gather():
+        def go(index, source, target, peer):
+            push(source, target, ag_send.at[index], ag_recv.at[index], peer)
 
         def come(index, ref):
             remote(ref, ref, ag_send.at[index], ag_recv.at[index], partner).wait_recv()
 
-        def block(x_, side):
-            return buf.at[:, rows(x_ * ROWS, ROWS), side]
+        def part(x_, z_):
+            return wq.at[:, x_ * Z + lax.rem(z_ + Z, Z), c]
+
+        def block(x_, core):
+            return wq.at[:, pl.ds(x_ * Z, Z), core]
 
         offsets = (0, -1, 1, -2, 2, -3, 3, 4)
 
         def across(g):
-            ref = part(buf, x, z + offsets[g], mine)
+            ref = part(x, z + offsets[g])
             for step in (1, 3, 2):
-                go(6 + 3 * g + step, ref, x_by(step))
-
-        own = part(buf, x, z, mine)
+                go(6 + 3 * g + step, wr if g == 0 else ref, ref, x_by(step))
+
         for g in range(1, Z):
-            go(g - 1, own, z_by(-offsets[g]))
+            go(g - 1, wr, part(x, z), z_by(-offsets[g]))
         across(0)
-        yield
+        wq[:, chip, c] = wr[...]
         for g in range(1, Z):
-            come(g - 1, part(buf, x, z + offsets[g], mine))
+            come(g - 1, part(x, z + offsets[g]))
             across(g)
-        go(31, block(x, mine), partner)
-        yield
+        go(31, block(x, c), block(x, c), partner)
         for step in (1, 3, 2):
             x_ = lax.rem(x + X - step, X)
             for g in range(Z):
-                come(6 + 3 * g + step, part(buf, x_, z + offsets[g], mine))
-            go(31 + step, block(x_, mine), partner)
+                come(6 + 3 * g + step, part(x_, z + offsets[g]))
+            go(31 + step, block(x_, c), block(x_, c), partner)
         for step in (0, 1, 3, 2):
-            come(31 + step, block(lax.rem(x + X - step, X), other))
-        yield
+            x_ = lax.rem(x + X - step, X)
+            come(31 + step, block(x_, o))
+            for w in range(3):
+                whole = wq[w, pl.ds(x_ * Z, Z)].astype(F32)
+                w0[w, rows(x_ * ROWS, ROWS), :] = whole.reshape(ROWS, D).astype(BF16)
 
     def reduce(partial):
         def go(index, source, target, peer):
@@ -219,6 +212,7 @@
         yield
         for j in range(Z):
             second(j)
+        yield
         sides = [fx[:, pl.ds(pl.multiple_of(c * 8, 8), 8), :], None]
         for j in range(Z - 1):
             for index in range(2):
@@ -279,7 +273,7 @@
                     w, 3 + step, sz.at[phase, w, rows(target * PIECE, PIECE), :],
                     qz.at[phase, w, step - 1], z_by(step),
                 )
-        yield
+            yield
         for w in range(3):
             result = xblk[w, rows(z * PIECE, PIECE), :]
             for step in (1, 7, 2, 6, 3, 5, 4):
@@ -326,7 +320,7 @@
         for _ in steps:
             pass
 
-    run(gather(w0))
+    gather()
     for load in loads[3:]:
         load.wait()
 
@@ -401,17 +395,18 @@
         ).astype(BF16)
 
     first_refs = [rf.at[w, pl.ds(0, T), :] for w in range(3)]
+    old = len(sent)
     steps = combine(fast_partial, 0, gh, 1.0)
     next(steps)
     next(steps)
     hidden_q = apply_forward(0, w0)
-    next(steps)
     lt[0, :, :T] = turned(q_ref[0])
     lt[1, :, :T] = turned(hidden_q)
+    q1_t[...] = turned(q_ref[1])
+    drain(old)
     next(steps)
     apply_backward(0, w0, first_refs)
-    next(steps)
-    q1_t[...] = turned(q_ref[1])
+    run(steps)
     finish(0, 0, gh)
 
     def schulz(w, carry):
@@ -454,14 +449,16 @@
         left_t = hq1_t[...] if w == 2 else q1_t[...]
         return mm(left_t, r1[w, :, side])
 
+    old = len(sent)
     steps = combine(second_partial, 1, pt, -1.0)
     next(steps)
     next(steps)
     query_grad(1, w1, second_refs)
-    next(steps)
     query_grad(0, w0, first_refs)
-    for _ in steps:
-        pass
+    drain(old)
+    for w in range(3):
+        leave(w, 0, gh)
+    run(steps)
     finish(0, 1, pt)
 
     def schulz_back(w, carry):
@@ -516,22 +513,24 @@
     def last_partial(w, side):
         return mm(lt[w // 2], rf[w, :, side])
 
+    old = len(sent)
     steps = reduce(last_partial)
+    next(steps)
     next(steps)
     gk_out[...] = (
         mt(rg[0], cc[0]) + mt(rg[1], cc[1]) + mt(rf[0, T:], w0[0]) + mt(rf[1, T:], w0[1])
     ).astype(BF16)
-    next(steps)
     gv_out[...] = (-mm(hid_k[...], cc[2]) - mm(r1[2], w0[2])).astype(BF16)
+    drain(old)
+    for w in range(3):
+        leave(w, 1, pt)
+    next(steps)
+    drain(3 + 3 * Z)
     run(steps)
 
     for w, out in enumerate((gg_out, gu_out, gd_out)):
         out[0] = fr[w]
-    for copy in sent:
-        copy.wait_send()
-    for phase, buf in enumerate((gh, pt)):
-        for w in range(3):
-            leave(w, phase, buf)
+    drain(len(sent))
 
 
 def hand_on(*refs):
@@ -553,7 +552,7 @@
     scratch = [
         pltpu.VMEM((2, T, D), BF16), pltpu.VMEM((T, D), BF16), pltpu.VMEM((T, D), BF16),
         pltpu.VMEM((2, T, D), BF16), pltpu.VMEM((1, D), F32), pltpu.VMEM((3, 8, D), BF16), dma((8,)),
-        pltpu.VMEM((3, 8, D), F32), pltpu.VMEM((3, PIECE, HALF), F32),
+        pltpu.VMEM((3, X * Z, 2, 8, D), BF16),
     ] + [square] * 5 + [pltpu.VMEM((3, D, 2 * D), BF16)] * 2 + [pltpu.VMEM((3, 2 * D, D), BF16)] * 2 + [
         wide, wide, wide, pltpu.VMEM((T, D), BF16), pltpu.VMEM((D, T), BF16),
         pltpu.VMEM((3, T, D), BF16),

time: 122 us -> 121 us (level)
    pallas_call x1, Pallas kernels: 120 us -> 119 us  [per_device(): pl.pallas_call(kernel, out_shape=tuple((pltpu.VMEM(shape.shape, shape.dty...]
where the time goes in v4:
time: 121 us; the launch traced here: 120 us
  Pallas kernels  120 us (99%)
    pallas_call x1, Pallas kernels, per_device(): pl.pallas_call(kernel, out_shape=tuple((pltpu.VMEM(shape.shape, shape.dty...  119 us

profile of v4, /device:TPU:1, one launch (start us, length us, event | category | flops | bytes accessed | tf_op | source)
XLA Modules:
  0.0 120.4 jit_solution(2304702393559961332)
XLA Ops:
  0.6 118.8 %shard_map.127 = (bf16[2,128,512]{2,1,0:T(8,128)(2,1)S(1)}, bf16[128,512]{1,0:T(8,128)(2,1)S(1)}, bf16[128,512]{1,0:T(8,128)(2,1)S(1)}, f32[1,8,512]{2,1,0:T(8,1...) custom-call(bf16[2,128,512]{2,1,0:T(8,128)(2,1)} %q_hbm.1, bf16[128,512]{1,0:T(8,128)(2,1)} %k_hbm.1, ...), custom_call_target="tpu_custom_call" | custom-call | tf_op jit(solution)/shard_map/pallas_call | solution.py:579
  119.4 0.8 shard_map.128

commit v5 on v4

--- a/solution.py
+++ b/solution.py
@@ -455,6 +455,14 @@
     next(steps)
     query_grad(1, w1, second_refs)
     query_grad(0, w0, first_refs)
+    gate_pre, up_pre, back = gk_s[...], uk_s[...], back_s[...]
+    sigma = sigmoid(gate_pre)
+    slope = sigma * (1.0 + gate_pre * (1.0 - sigma))
+    curve = sigma * (1.0 - sigma) * (2.0 + gate_pre * (1.0 - 2.0 * sigma))
+    oq[...] = gate_pre * sigma
+    gq_s[...] = back * slope
+    uq_s[...] = back * up_pre * curve
+    uk_s[...] = up_pre * slope
     drain(old)
     for w in range(3):
         leave(w, 0, gh)
@@ -497,16 +505,9 @@
     keys, values = k_ref[...], v_ref[...]
     along_gate, along_up = mm(keys, cc[0]), mm(keys, cc[1])
     along_hidden = -mt(values, cc[2])
-    gate_pre, up_pre, back = gk_s[...], uk_s[...], back_s[...]
-    sigma = sigmoid(gate_pre)
-    active = gate_pre * sigma
-    slope = sigma * (1.0 + gate_pre * (1.0 - sigma))
-    curve = sigma * (1.0 - sigma) * (2.0 + gate_pre * (1.0 - 2.0 * sigma))
-    d_back = (along_gate * up_pre * slope + along_up * active).astype(BF16)
-    rf[1, T:] = (along_gate * back * slope + along_hidden * active).astype(BF16)
-    rf[0, T:] = (
-        along_gate * back * up_pre * curve + along_up * back * slope + along_hidden * up_pre * slope
-    ).astype(BF16)
+    d_back = (along_gate * uk_s[...] + along_up * oq[...]).astype(BF16)
+    rf[1, T:] = (along_gate * gq_s[...] + along_hidden * oq[...]).astype(BF16)
+    rf[0, T:] = (along_gate * uq_s[...] + along_up * gq_s[...] + along_hidden * uk_s[...]).astype(BF16)
     lt[1, :, T:] = turned(-d_back.astype(F32))
     r1[2] = d_back
 

time: 121 us -> 120 us (level)
  no operation moved by 1% of the time
where the time goes in v5:
time: 120 us
  Pallas kernels  120 us (100%)
    pallas_call x1, Pallas kernels, per_device(): pl.pallas_call(kernel, out_shape=tuple((pltpu.VMEM(shape.shape, shape.dty...  119 us

profile of v5, /device:TPU:1, one launch (start us, length us, event | category | flops | bytes accessed | tf_op | source)
XLA Modules:
  0.0 120.4 jit_solution(9970985789011521596)
XLA Ops:
  0.6 118.7 %shard_map.127 = (bf16[2,128,512]{2,1,0:T(8,128)(2,1)S(1)}, bf16[128,512]{1,0:T(8,128)(2,1)S(1)}, bf16[128,512]{1,0:T(8,128)(2,1)S(1)}, f32[1,8,512]{2,1,0:T(8,1...) custom-call(bf16[2,128,512]{2,1,0:T(8,128)(2,1)} %q_hbm.1, bf16[128,512]{1,0:T(8,128)(2,1)} %k_hbm.1, ...), custom_call_target="tpu_custom_call" | custom-call | tf_op jit(solution)/shard_map/pallas_call | solution.py:580
  119.4 0.8 shard_map.128
